TPU v7x, 512 devices: a whole 4x4x16 slice. The times are simulated.
512 devices in a mesh: row: 32 (over x, z_lo, core), col: 16 (over y, z_hi).
Axes of the slice: x: 4, y: 4, z: 16 (z_hi: 4, z_lo: 4; z = z_hi * 4 + z_lo), core: 2. Of those that a mesh axis runs over, the one named last changes fastest.
Arguments:
- amplitudes: bfloat16 [2, 2048, 2048], P(None, 'row', 'col'), may hold values from -6 to 6
- factor: bfloat16 [2048, 4096], P('row', 'col'), may hold values from -0.125 to 0.125
- kernel: float32 [4096, 4096], P('row', 'col'), may hold values from -6 to 6
Outputs:
- ladder: bfloat16 [2, 2048, 2048], P(None, 'row', 'col')
All inputs are finite; a program needn't handle non-finite values.
Results may differ from a plain program's by a relative error of at most 0.015.
Values may be sent and summed in bfloat16 or wider, within the bound.
A program may use at most 64 MiB of HBM per device.

v0:
```python
import jax
import jax.numpy as jnp
from jax import lax
from jax.sharding import PartitionSpec as P


def in_order(parts, dim):
    parts = jnp.moveaxis(parts, 0, dim)
    shape = parts.shape
    return parts.reshape(*shape[:dim], shape[dim] * shape[dim + 1], *shape[dim + 2 :])


def sent_to_all(value, axis):
    copies = jnp.broadcast_to(value, (lax.axis_size(axis), *value.shape))
    return lax.all_to_all(copies, axis, split_axis=0, concat_axis=0, tiled=True)


def gathered_copies(value, axis, dim):
    return in_order(sent_to_all(value, axis), dim)


def cut_along(value, dim, size):
    shape = value.shape
    parts = value.reshape(*shape[:dim], size, shape[dim] // size, *shape[dim + 1 :])
    return jnp.moveaxis(parts, dim, 0)


def sent_and_summed(value, axis, dim):
    size = lax.axis_size(axis)
    parts = lax.all_to_all(cut_along(value, dim, size), axis, 0, 0, tiled=True)
    return jnp.sum(parts.astype(jnp.float32), axis=0)


def per_device(amplitudes, factor, kernel):
    factor_cols = gathered_copies(factor, "row", 0)
    factor_rows = gathered_copies(factor, "col", 1)
    factor_first = lax.all_to_all(factor_rows, "row", split_axis=1, concat_axis=0, tiled=True)
    factor_part = factor_cols
    projected = jnp.einsum(
        "pak,kq->paq",
        gathered_copies(amplitudes, "col", 2),
        factor_part,
        preferred_element_type=jnp.float32,
    ).astype(jnp.bfloat16)
    factor_part = factor_first
    grid_pairs = jnp.einsum(
        "kp,nkq->npq",
        factor_part,
        gathered_copies(projected, "row", 1),
        preferred_element_type=jnp.float32,
    )
    scaled = (kernel[None] * grid_pairs).astype(jnp.bfloat16)
    factor_part = factor_cols
    half_back = sent_and_summed(
        jnp.einsum("bq,npq->bnp", factor_part, scaled, preferred_element_type=jnp.float32).astype(
            jnp.bfloat16
        ),
        "col",
        0,
    )
    half_back = half_back.astype(jnp.bfloat16)
    factor_part = factor_rows
    result = jnp.einsum(
        "ak,bnk->nab",
        factor_part,
        gathered_copies(half_back, "row", 2),
        preferred_element_type=jnp.float32,
    )
    return result.astype(jnp.bfloat16)


def solution(mesh):
    placed = (P(None, "row", "col"), P("row", "col"), P("row", "col"))
    return jax.shard_map(
        per_device, mesh=mesh, in_specs=placed, out_specs=P(None, "row", "col"), check_vma=False
    )
```

profile of v0, /device:TPU:6, one launch (start us, length us, event | category | flops | bytes accessed | tf_op | source)
XLA Modules:
  0.0 320.6 jit_solution(5627007424775163365)
XLA Ops:
  0.0 0.0 copy-start.3
  0.0 0.9 broadcast_in_dim.16
  0.9 45.2 %all_to_all.46 = bf16[16,2,64,128]{3,2,1,0:T(8,128)(2,1)S(1)} all-to-all(bf16[16,2,64,128]{3,2,1,0:T(8,128)(2,1)S(1)} %broadcast_in_dim.16), channel_id=1, replica_groups=mesh['row'=32,'col'=16] {'col'}, dimensions={0} | all-to-all | bytes 1048576 | tf_op jit(solution)/shard_map/all_to_all | solution.py:15
  46.1 0.8 broadcast_in_dim.19
  46.9 30.2 %all_to_all.47 = bf16[16,64,256]{2,1,0:T(8,128)(2,1)S(1)} all-to-all(bf16[16,64,256]{2,1,0:T(8,128)(2,1)S(1)} %broadcast_in_dim.19), channel_id=1, replica_groups=mesh['row'=32,'col'=16] {'col'}, dimensions={0} | all-to-all | bytes 1048576 | tf_op jit(solution)/shard_map/all_to_all | solution.py:15
  77.1 0.0 copy-done.3
  77.1 1.1 broadcast_in_dim.17
  78.2 19.4 %all-to-all-start.1 = ((bf16[32,64,256]{2,1,0:T(8,128)(2,1)}), bf16[32,64,256]{2,1,0:T(8,128)(2,1)S(1)}, u32[]{:S(2)}, u32[]{:S(2)}) async-start(bf16[32,64,256]{2,1,0:T(8,128)(2,1)} %broadcast_in_dim.17), calls=%async_computation.1 | async-start | bytes 2097152 | tf_op jit(solution)/shard_map/all_to_all | solution.py:15
  97.6 0.3 copy.14
  97.9 0.0 copy-start
  97.9 0.2 all_to_all.34
  98.1 1.0 copy.15
  99.2 24.1 %all-to-all-done.1 = bf16[32,64,256]{2,1,0:T(8,128)(2,1)S(1)} async-done(((bf16[32,64,256]{2,1,0:T(8,128)(2,1)}), bf16[32,64,256]{2,1,0:T(8,128)(2,1)S(1)}, u32[]{:S(2)}, u32[]{:S(2)}) %all-to-all-start.1) | async-done | bytes 1048608 | tf_op jit(solution)/shard_map/all_to_all | solution.py:15
  123.2 6.1 %all-to-all-start.4 = ((bf16[64,32,128]{2,0,1:T(8,128)(2,1)}), bf16[64,32,128]{2,0,1:T(8,128)(2,1)S(1)}, u32[]{:S(2)}, u32[]{:S(2)}) async-start(bf16[64,32,128]{2,0,1:T(8,128)(2,1)} %copy.15), calls=%async_computation.4 | async-start | bytes 1048576 | tf_op jit(solution)/shard_map/all_to_all | solution.py:37
  129.4 0.3 convolution_convert_fusion.1
  129.7 0.0 copy-done
  129.7 14.0 %all-to-all-done.4 = bf16[64,32,128]{2,0,1:T(8,128)(2,1)S(1)} async-done(((bf16[64,32,128]{2,0,1:T(8,128)(2,1)}), bf16[64,32,128]{2,0,1:T(8,128)(2,1)S(1)}, u32[]{:S(2)}, u32[]{:S(2)}) %all-to-all-start.4) | async-done | bytes 524320 | tf_op jit(solution)/shard_map/all_to_all | solution.py:37
  143.7 0.0 copy-start.2
  143.7 1.6 broadcast_in_dim.18
  145.3 0.0 copy-start.4
  145.3 0.0 copy-done.2
  145.3 6.4 %all-to-all-start.2 = ((bf16[32,2,64,256]{3,2,1,0:T(8,128)(2,1)}), bf16[32,2,64,256]{3,2,1,0:T(8,128)(2,1)S(1)}, u32[]{:S(2)}, u32[]{:S(2)}) async-start(bf16[32,2,64,256]{3,2,1,0:T(8,128)(2,1)} %broadcast_in_dim.18), calls=%async_computation.2 | async-start | bytes 4194304 | tf_op jit(solution)/shard_map/all_to_all | solution.py:15
  151.7 0.0 copy-done.4
  151.7 0.1 copy.12
  151.8 48.0 %all-to-all-done.2 = bf16[32,2,64,256]{3,2,1,0:T(8,128)(2,1)S(1)} async-done(((bf16[32,2,64,256]{3,2,1,0:T(8,128)(2,1)}), bf16[32,2,64,256]{3,2,1,0:T(8,128)(2,1)S(1)}, u32[]{:S(2)}, u32[]{:S(2)}) %all-to-all-start.2) | async-done | bytes 2097184 | tf_op jit(solution)/shard_map/all_to_all | solution.py:15
  199.8 3.7 %fusion.5 = bf16[2,16,16,8,128]{4,3,2,1,0:T(8,128)(2,1)} fusion(bf16[2048,256,1]{1,0,2:T(8,128)(2,1)S(1)} %bitcast.65, bf16[32,2,64,256]{3,2,1,0:T(8,128)(2,1)S(1)} %all-to-all-done.2, bf16[64,32,128]{2,0,1:T(8,128)(2,1)} %copy-done.2, f32[128,256]{0,1:T(8,128)S(1)} %copy.12), kind=kOutput, calls=%fused_computation.6 | convolution fusion | flops 537526272 | bytes 4849664 | tf_op jit(solution)/shard_map/bq,npq->bnp/dot_general | solution.py:55
  203.5 1.5 copy.41
  205.0 54.9 %all_to_all.48 = bf16[16,128,2,128]{1,3,2,0:T(8,128)(2,1)S(1)} all-to-all(bf16[16,128,2,128]{1,3,2,0:T(8,128)(2,1)S(1)} %bitcast.66), channel_id=1, replica_groups=mesh['row'=32,'col'=16] {'col'}, dimensions={0} | all-to-all | bytes 2097152 | tf_op jit(solution)/shard_map/all_to_all | solution.py:30
  259.9 0.1 reduce_sum.12
  260.1 0.1 copy.19
  260.2 1.8 broadcast_in_dim.20
  262.0 0.0 copy-start.1
  262.1 9.1 %all-to-all-start.6 = ((bf16[32,128,2,128]{3,1,2,0:T(8,128)(2,1)}), bf16[32,128,2,128]{3,1,2,0:T(8,128)(2,1)S(1)}, u32[]{:S(2)}, u32[]{:S(2)}) async-start(bf16[32,128,2,128]{3,1,2,0:T(8,128)(2,1)} %broadcast_in_dim.20), calls=%async_computation.6 | async-start | bytes 4194304 | tf_op jit(solution)/shard_map/all_to_all | solution.py:15
  271.2 0.0 copy-done.1
  271.2 0.2 reshape.29
  271.4 47.8 %all-to-all-done.6 = bf16[32,128,2,128]{3,1,2,0:T(8,128)(2,1)S(1)} async-done(((bf16[32,128,2,128]{3,1,2,0:T(8,128)(2,1)}), bf16[32,128,2,128]{3,1,2,0:T(8,128)(2,1)S(1)}, u32[]{:S(2)}, u32[]{:S(2)}) %all-to-all-start.6) | async-done | bytes 2097184 | tf_op jit(solution)/shard_map/all_to_all | solution.py:15
  319.3 1.4 fusion.18
Async XLA Ops:
  0.0 77.1 %copy-start.3 = (bf16[64,256]{1,0:T(8,128)(2,1)S(1)}, bf16[64,256]{1,0:T(8,128)(2,1)}, u32[]{:S(2)}) copy-start(bf16[64,256]{1,0:T(8,128)(2,1)} %param.4) | copy-start | bytes 98308
  78.2 45.0 %all-to-all-start.1 = ((bf16[32,64,256]{2,1,0:T(8,128)(2,1)}), bf16[32,64,256]{2,1,0:T(8,128)(2,1)S(1)}, u32[]{:S(2)}, u32[]{:S(2)}) async-start(bf16[32,64,256]{2,1,0:T(8,128)(2,1)} %broadcast_in_dim.17), calls=%async_computation.1 | async-start | bytes 2097152 | tf_op jit(solution)/shard_map/all_to_all | solution.py:15
  97.9 31.7 %copy-start = (bf16[64,16,256]{2,1,0:T(8,128)(2,1)}, bf16[64,16,256]{2,1,0:T(8,128)(2,1)S(1)}, u32[]{:S(2)}) copy-start(bf16[64,16,256]{2,1,0:T(8,128)(2,1)S(1)} %copy.14) | copy-start | bytes 1572868
  123.2 20.5 %all-to-all-start.4 = ((bf16[64,32,128]{2,0,1:T(8,128)(2,1)}), bf16[64,32,128]{2,0,1:T(8,128)(2,1)S(1)}, u32[]{:S(2)}, u32[]{:S(2)}) async-start(bf16[64,32,128]{2,0,1:T(8,128)(2,1)} %copy.15), calls=%async_computation.4 | async-start | bytes 1048576 | tf_op jit(solution)/shard_map/all_to_all | solution.py:37
  143.7 1.6 copy-start.2
  145.3 6.4 %copy-start.4 = (f32[128,256]{1,0:T(8,128)S(1)}, f32[128,256]{1,0:T(8,128)}, u32[]{:S(2)}) copy-start(f32[128,256]{1,0:T(8,128)} %param.5) | copy-start | bytes 393220
  145.3 54.5 %all-to-all-start.2 = ((bf16[32,2,64,256]{3,2,1,0:T(8,128)(2,1)}), bf16[32,2,64,256]{3,2,1,0:T(8,128)(2,1)S(1)}, u32[]{:S(2)}, u32[]{:S(2)}) async-start(bf16[32,2,64,256]{3,2,1,0:T(8,128)(2,1)} %broadcast_in_dim.18), calls=%async_computation.2 | async-start | bytes 4194304 | tf_op jit(solution)/shard_map/all_to_all | solution.py:15
  262.0 9.1 %copy-start.1 = (bf16[64,16,256]{2,1,0:T(8,128)(2,1)S(1)}, bf16[64,16,256]{2,1,0:T(8,128)(2,1)}, u32[]{:S(2)}) copy-start(bf16[64,16,256]{2,1,0:T(8,128)(2,1)} %copy-done) | copy-start | bytes 1572868
  262.1 57.2 %all-to-all-start.6 = ((bf16[32,128,2,128]{3,1,2,0:T(8,128)(2,1)}), bf16[32,128,2,128]{3,1,2,0:T(8,128)(2,1)S(1)}, u32[]{:S(2)}, u32[]{:S(2)}) async-start(bf16[32,128,2,128]{3,1,2,0:T(8,128)(2,1)} %broadcast_in_dim.20), calls=%async_computation.6 | async-start | bytes 4194304 | tf_op jit(solution)/shard_map/all_to_all | solution.py:15
where the time goes:
time: 324 us; the launch traced here: 321 us
  waiting for transfers between devices  134 us (41%)
  blocking collectives  130 us (40%)
  starting transfers between devices  41.1 us (13%)
  local copies, waits for them, and re-layouts  9.69 us (3%)
  matrix products  5.35 us (2%)
    all_to_all x3, waiting for transfers between devices, sent_to_all(): return lax.all_to_all(copies, axis, split_axis=0, concat_axis=0, tiled=True)  120 us
    all_to_all x2, blocking collectives, sent_to_all(): return lax.all_to_all(copies, axis, split_axis=0, concat_axis=0, tiled=True)  75.4 us
    all_to_all x1, blocking collectives, sent_and_summed(): parts = lax.all_to_all(cut_along(value, dim, size), axis, 0, 0, tiled=True)  54.9 us
    all_to_all x3, starting transfers between devices, sent_to_all(): return lax.all_to_all(copies, axis, split_axis=0, concat_axis=0, tiled=True)  34.9 us
    all_to_all x1, waiting for transfers between devices, per_device(): lax.all_to_all(factor_rows, 'row', split_axis=1, concat_axis=0, tiled=True)  14 us
  transfers between devices with their start and end apart: 4, of which 4 were waited for; matrix products, arithmetic and copies ran while one was open for 1% of the time, Pallas kernels for 0%

commit v1 on v0

v1 whole, which is shorter than its diff:
```python
import jax
import jax.numpy as jnp
from jax import lax
from jax.experimental import pallas as pl
from jax.experimental.pallas import tpu as pltpu
from jax.sharding import PartitionSpec as P

MESH = pl.DeviceIdType.MESH
F32, BF16 = jnp.float32, jnp.bfloat16
N = 4
DS = (1, 3, 2)


def dot(a, b, dims):
    return lax.dot_general(a, b, (dims, ((), ())), preferred_element_type=F32)


def kernel(
    a_ref, x_ref, k_ref, out_ref,
    kv, ag, xq, xp, tg, gacc, gr, wb, us, urx, us2, urz, osd, ory, os2, orz,
    lsem, s1, s2, s3, s4, s5, s6, s7, s8, s9, s10, sg, s11, s12, s13, s14,
):
    row, col = lax.axis_index("row"), lax.axis_index("col")
    k = lax.rem(row, 2)
    R = lax.div(row, 2)
    x, zl = lax.div(R, N), lax.rem(R, N)
    y, zh = lax.div(col, N), lax.rem(col, N)
    C = col

    def at(x=x, zl=zl, k=k, y=y, zh=zh):
        return ((x * N + zl) * 2 + k, y * N + zh)

    def plus(v, d):
        return lax.rem(v + d, N)

    mate = at(k=1 - k)
    flip = at(x=y, zl=zh, y=x, zh=zl)
    off_diagonal = R != C

    def remote(src, dst, sems, index, device):
        return pltpu.make_async_remote_copy(
            src_ref=src, dst_ref=dst, send_sem=sems.at[(0, *index)], recv_sem=sems.at[(1, *index)],
            device_id=device, device_id_type=MESH,
        )

    started = []

    def send(*args):
        copy = remote(*args)
        copy.start()
        started.append(copy)
        return copy

    own_a = pltpu.make_async_copy(a_ref, ag.at[C], lsem.at[0])
    own_x = pltpu.make_async_copy(x_ref, xq.at[R, k], lsem.at[1])
    own_k = pltpu.make_async_copy(k_ref, kv, lsem.at[2])
    own_p = pltpu.make_async_copy(x_ref, xp.at[R], lsem.at[3])
    for copy in (own_a, own_x, own_k):
        copy.start()

    barrier = pltpu.get_barrier_semaphore()
    partners = [mate]
    for d in DS:
        partners += [at(x=plus(x, d)), at(zl=plus(zl, d)), at(y=plus(y, d)), at(zh=plus(zh, d))]
    for device in partners:
        pl.semaphore_signal(barrier, inc=1, device_id=device, device_id_type=MESH)

    @pl.when(off_diagonal)
    def _():
        pl.semaphore_signal(barrier, inc=1, device_id=flip, device_id_type=MESH)
        pl.semaphore_wait(barrier, len(partners) + 1)

    @pl.when(jnp.logical_not(off_diagonal))
    def _():
        pl.semaphore_wait(barrier, len(partners))

    own_a.wait()
    own_x.wait()
    flipped = remote(x_ref, xp.at[R], s6, (0,), flip)
    a_z = {d: send(ag.at[C], ag.at[C], s1, (d,), at(zh=plus(zh, d))) for d in DS}
    x_z = {d: send(xq.at[R, k], xq.at[R, k], s3, (d,), at(zl=plus(zl, d))) for d in DS}

    def spread_a(dz):
        block = ag.at[y * N + plus(zh, N - dz)]
        return {d: send(block, block, s2, (dz, d), at(y=plus(y, d))) for d in DS}

    def spread_x(dz):
        block = xq.at[x * N + plus(zl, N - dz), k]
        return {d: send(block, block, s4, (dz, d), at(x=plus(x, d))) for d in DS}

    a_y, x_x = {}, {}
    a_y[0] = spread_a(0)
    x_x[0] = spread_x(0)

    @pl.when(off_diagonal)
    def _():
        flipped.start()

    @pl.when(jnp.logical_not(off_diagonal))
    def _():
        own_p.start()

    for dz in DS:
        x_z[dz].wait_recv()
        x_x[dz] = spread_x(dz)

    def share_x(dx):
        blocks = xq.at[pl.ds(plus(x, N - dx) * N, N), k]
        return send(blocks, blocks, s5, (dx,), mate)

    x_k = {0: share_x(0)}
    for dz in DS:
        a_z[dz].wait_recv()
        a_y[dz] = spread_a(dz)
    for dx in DS:
        for dz in (0, *DS):
            x_x[dz][dx].wait_recv()
        x_k[dx] = share_x(dx)

    for dx in (0, *DS):
        x_k[dx].wait_recv()
    acc = jnp.zeros((128, 256), F32)
    for dy in (0, *DS):
        ys = plus(y, N - dy)
        if dy:
            for dz in (0, *DS):
                a_y[dz][dy].wait_recv()
        for h in range(N):
            block = xq[ys * N + h].reshape(128, 256)
            acc += dot(ag[ys * N + h], block, ((1,), (0,)))
    tg[R, :, 0:256] = acc[0:64].astype(BF16)
    tg[R, :, 256:512] = acc[64:128].astype(BF16)

    t_z = {d: send(tg.at[R], tg.at[R], s9, (d,), at(zl=plus(zl, d))) for d in DS}

    def spread_t(dz):
        block = tg.at[x * N + plus(zl, N - dz)]
        return {d: send(block, block, s10, (dz, d), at(x=plus(x, d))) for d in DS}

    t_x = {0: spread_t(0)}

    @pl.when(off_diagonal)
    def _():
        flipped.wait_send()
        flipped.wait_recv()

    @pl.when(jnp.logical_not(off_diagonal))
    def _():
        own_p.wait()

    p_z = {d: send(xp.at[C], xp.at[C], s7, (d,), at(zh=plus(zh, d))) for d in DS}

    def spread_p(dz):
        block = xp.at[y * N + plus(zh, N - dz)]
        return {d: send(block, block, s8, (dz, d), at(y=plus(y, d))) for d in DS}

    p_y = {0: spread_p(0)}
    for dz in DS:
        t_z[dz].wait_recv()
        t_x[dz] = spread_t(dz)
    for dz in DS:
        p_z[dz].wait_recv()
        p_y[dz] = spread_p(dz)
    for dz in (0, *DS):
        for dy in DS:
            p_y[dz][dy].wait_recv()

    acc = jnp.zeros((256, 512), F32)
    for dx in (0, *DS):
        xs = plus(x, N - dx) * N
        if dx:
            for dz in (0, *DS):
                t_x[dz][dx].wait_recv()
        left = xp[pl.ds(xs, N)].reshape(256, 256)
        right = tg[pl.ds(xs, N)].reshape(256, 512)
        acc += dot(left, right, ((0,), (0,)))
    gacc[...] = acc
    mine, theirs = pl.ds(k * 128, 128), pl.ds((1 - k) * 128, 128)
    send(gacc.at[theirs], gr, sg, (0,), mate).wait_recv()
    own_k.wait()
    kern = kv[...]
    for p in range(2):
        half = slice(p * 256, p * 256 + 256)
        wb[mine, half] = (kern * (gacc[mine, half] + gr[:, half])).astype(BF16)
    send(wb.at[mine], wb.at[mine], sg, (1,), mate).wait_recv()

    w = wb[...]
    u_x = {}
    for dx in (*DS, 0):
        xs = plus(x, dx) * N
        part = dot(xp[pl.ds(xs, N)].reshape(256, 256), w, ((1,), (0,)))
        if dx:
            us[dx] = part.reshape(N, 64, 512).astype(BF16)
            u_x[dx] = send(us.at[dx], urx.at[dx], s11, (dx,), at(x=plus(x, dx)))
    us2[...] = part.reshape(N, 64, 512)
    for dx in DS:
        u_x[dx].wait_recv()
        us2[...] += urx[dx].astype(F32)
    u_z = {}
    for d in DS:
        us[0, d] = us2[plus(zl, d)].astype(BF16)
        u_z[d] = send(us.at[0, d], urz.at[d], s12, (d,), at(zl=plus(zl, d)))
    total = us2[zl]
    for d in DS:
        u_z[d].wait_recv()
        total += urz[d].astype(F32)
    total = total.astype(BF16)
    left = jnp.concatenate([total[:, 0:256], total[:, 256:512]], axis=0)

    o_y = {}
    for dy in (*DS, 0):
        ys = plus(y, dy) * N
        for h in range(N):
            part = dot(left, xq[ys + h].reshape(128, 256), ((1,), (1,)))
            if dy:
                osd[dy, h] = part.astype(BF16)
            else:
                os2[h] = part
        if dy:
            o_y[dy] = send(osd.at[dy], ory.at[dy], s13, (dy,), at(y=plus(y, dy)))
    for dy in DS:
        o_y[dy].wait_recv()
        os2[...] += ory[dy].astype(F32)
    o_z = {}
    for d in DS:
        osd[0, d] = os2[plus(zh, d)].astype(BF16)
        o_z[d] = send(osd.at[0, d], orz.at[d], s14, (d,), at(zh=plus(zh, d)))
    total = os2[zh]
    for d in DS:
        o_z[d].wait_recv()
        total += orz[d].astype(F32)
    out_ref[...] = total.astype(BF16)
    for copy in started:
        copy.wait_send()


def per_device(amplitudes, factor, kern):
    any_spec = pl.BlockSpec(memory_space=pl.ANY)
    vmem = pltpu.VMEM
    dma = pltpu.SemaphoreType.DMA
    result = pl.pallas_call(
        kernel,
        name="ladder",
        out_shape=jax.ShapeDtypeStruct((128, 128), BF16),
        in_specs=[any_spec] * 3,
        out_specs=pl.BlockSpec(memory_space=vmem),
        scratch_shapes=[
            vmem((128, 256), F32),
            vmem((16, 128, 128), BF16),
            vmem((16, 2, 64, 256), BF16),
            vmem((16, 64, 256), BF16),
            vmem((16, 64, 512), BF16),
            vmem((256, 512), F32),
            vmem((128, 512), F32),
            vmem((256, 512), BF16),
            vmem((4, 4, 64, 512), BF16),
            vmem((4, 4, 64, 512), BF16),
            vmem((4, 64, 512), F32),
            vmem((4, 64, 512), BF16),
            vmem((4, 4, 128, 128), BF16),
            vmem((4, 4, 128, 128), BF16),
            vmem((4, 128, 128), F32),
            vmem((4, 128, 128), BF16),
            dma((4,)),
            dma((2, 4)), dma((2, 4, 4)), dma((2, 4)), dma((2, 4, 4)), dma((2, 4)), dma((2, 1)),
            dma((2, 4)), dma((2, 4, 4)), dma((2, 4)), dma((2, 4, 4)), dma((2, 2)), dma((2, 4)),
            dma((2, 4)), dma((2, 4)), dma((2, 4)),
        ],
        compiler_params=pltpu.CompilerParams(collective_id=0, has_side_effects=True),
    )(amplitudes.reshape(128, 128), factor, kern)
    return result.reshape(2, 64, 128)


def solution(mesh):
    placed = (P(None, "row", "col"), P("row", "col"), P("row", "col"))
    return jax.shard_map(
        per_device, mesh=mesh, in_specs=placed, out_specs=P(None, "row", "col"), check_vma=False
    )
```

time: 324 us -> 96.8 us (0.30)
  the two profiles are of different devices: /device:TPU:6 before, /device:TPU:26 now
where the time goes in v1:
time: 96.8 us; the launch traced here: 96.7 us
  Pallas kernels  95.3 us (98%)
  local copies, waits for them, and re-layouts  1.38 us (1%)
    pallas_call x1, Pallas kernels, per_device(): pl.pallas_call(kernel, name='ladder', out_shape=jax.ShapeDtypeStruct((128...  95.3 us

profile of v1, /device:TPU:26, one launch (start us, length us, event | category | flops | bytes accessed | tf_op | source)
XLA Modules:
  0.0 96.7 jit_solution(8674018867387706474)
XLA Ops:
  0.0 95.3 %ladder.1 = bf16[128,128]{1,0:T(8,128)(2,1)} custom-call(bf16[128,128]{1,0:T(8,128)(2,1)} %bitcast.3, bf16[64,256]{1,0:T(8,128)(2,1)} %x_ref.1, f32[128,256]{1,0:T(8,128)} %k_ref.1), custom_call_target="tpu_custom_call" | custom-call | tf_op jit(solution)/shard_map/ladder/pallas_call | solution.py:241
  95.3 1.4 %copy.5 = bf16[2,64,128]{2,1,0:T(8,128)(2,1)} copy(bf16[2,64,128]{2,1,0:T(8,128)(2,1)} %bitcast.2) | data formatting | bytes 65536

commit v2 on v0

v2 whole, which is shorter than its diff:
```python
import jax
import jax.numpy as jnp
from jax import lax
from jax.experimental import pallas as pl
from jax.experimental.pallas import tpu as pltpu
from jax.sharding import PartitionSpec as P

MESH = pl.DeviceIdType.MESH
F32, BF16 = jnp.float32, jnp.bfloat16
N = 4
DS = (1, 3, 2)
COPIES = 240


def dot(a, b, dims):
    return lax.dot_general(a, b, (dims, ((), ())), preferred_element_type=F32)


def kernel(
    a_ref, x_ref, k_ref, out_ref,
    kv, ag, xq, xf, xp, tg, gacc, gr, wb, us, urx, us2, urz, osd, ory, os2, orz, lsem, sems,
):
    row, col = lax.axis_index("row"), lax.axis_index("col")
    k = lax.rem(row, 2)
    R = lax.div(row, 2)
    x, zl = lax.div(R, N), lax.rem(R, N)
    y, zh = lax.div(col, N), lax.rem(col, N)
    C = col

    def at(x=x, zl=zl, k=k, y=y, zh=zh):
        return ((x * N + zl) * 2 + k, y * N + zh)

    def plus(v, d):
        return lax.rem(v + d, N)

    def minus(v, d):
        return lax.rem(v + N - d, N)

    mate = at(k=1 - k)
    flip = at(x=y, y=x)
    up, down = at(zh=plus(zh, 1)), at(zh=plus(zh, 3))
    swaps = x != y
    root = zl == zh

    used = [0]
    started = []

    def remote(src, dst, device):
        index = used[0]
        used[0] += 1
        return pltpu.make_async_remote_copy(
            src_ref=src, dst_ref=dst, send_sem=sems.at[0, index], recv_sem=sems.at[1, index],
            device_id=device, device_id_type=MESH,
        )

    def send(src, dst, device):
        copy = remote(src, dst, device)
        copy.start()
        started.append(copy)
        return copy

    def otherwise(condition):
        return pl.when(jnp.logical_not(condition))

    own_a = pltpu.make_async_copy(a_ref, ag.at[:, C], lsem.at[0])
    own_x = pltpu.make_async_copy(x_ref, xq.at[R, k], lsem.at[1])
    own_k = pltpu.make_async_copy(k_ref, kv, lsem.at[2])
    own_f = pltpu.make_async_copy(x_ref, xf, lsem.at[3])
    own_p = pltpu.make_async_copy(xf, xp.at[y * N + zl], lsem.at[4])
    for copy in (own_a, own_x, own_k):
        copy.start()

    barrier = pltpu.get_barrier_semaphore()
    partners = [up, down, mate]
    for d in DS:
        partners += [at(x=plus(x, d)), at(zl=plus(zl, d)), at(y=plus(y, d))]
    for device in partners:
        pl.semaphore_signal(barrier, inc=1, device_id=device, device_id_type=MESH)

    @pl.when(swaps)
    def _():
        pl.semaphore_signal(barrier, inc=1, device_id=flip, device_id_type=MESH)
        pl.semaphore_wait(barrier, len(partners) + 1)

    @otherwise(swaps)
    def _():
        own_f.start()
        pl.semaphore_wait(barrier, len(partners))

    own_a.wait()
    own_x.wait()

    def a_block(p, dz):
        return ag.at[p, y * N + minus(zh, dz)]

    a_z, a_y, x_x = {}, {}, {}

    def spread_a(p, dz):
        block = a_block(p, dz)
        for d in DS:
            a_y[p, dz, d] = send(block, block, at(y=plus(y, d)))

    def spread_x(dz):
        block = xq.at[x * N + minus(zl, dz), k]
        for d in DS:
            x_x[dz, d] = send(block, block, at(x=plus(x, d)))

    def pass_a(p, dz, ahead):
        block = a_block(p, dz)
        return send(block, block, up if ahead else down)

    a_up, a_down, a_far = {}, {}, {}
    a_up[0], a_down[0] = pass_a(0, 0, True), pass_a(0, 0, False)
    x_z = {d: send(xq.at[R, k], xq.at[R, k], at(zl=plus(zl, d))) for d in DS}
    a_down[1], a_up[1] = pass_a(1, 0, False), pass_a(1, 0, True)
    spread_a(0, 0)
    spread_x(0)
    flipped = remote(x_ref, xf, flip)

    @pl.when(swaps)
    def _():
        flipped.start()

    spread_a(1, 0)
    for dz in DS:
        x_z[dz].wait_recv()
        spread_x(dz)

    a_up[0].wait_recv()
    a_far[0] = pass_a(0, 1, True)
    spread_a(0, 1)
    a_down[0].wait_recv()
    spread_a(0, 3)
    a_down[1].wait_recv()
    a_far[1] = pass_a(1, 3, False)
    a_up[1].wait_recv()

    @pl.when(swaps)
    def _():
        flipped.wait_send()
        flipped.wait_recv()

    @otherwise(swaps)
    def _():
        own_f.wait()

    mine_p = [pl.ds(y * N, 2), pl.ds(y * N + 2, 2)]
    collect = {d: remote(xf, xp.at[y * N + zl], at(zl=zh)) for d in DS}

    for d in DS:
        @pl.when(minus(zl, zh) == d)
        def _():
            collect[d].start()

    @pl.when(root)
    def _():
        own_p.start()

    spread_a(1, 3)
    spread_a(1, 1)

    def share_x(dx):
        blocks = xq.at[pl.ds(minus(x, dx) * N, N), k]
        return send(blocks, blocks, mate)

    x_k = {0: share_x(0)}
    for dx in DS:
        for dz in (0, *DS):
            x_x[dz, dx].wait_recv()
        x_k[dx] = share_x(dx)

    a_far[0].wait_recv()
    spread_a(0, 2)
    a_far[1].wait_recv()
    spread_a(1, 2)

    low = [remote(xp.at[s], xp.at[s], up) for s in mine_p]
    high = [remote(xp.at[s], xp.at[s], down) for s in mine_p]
    turn = minus(zh, zl)

    @pl.when(root)
    def _():
        own_p.wait()
        for d in DS:
            collect[d].wait_recv()
        low[0].start()
        high[1].start()
        low[1].start()
        high[0].start()

    def project(p):
        acc = jnp.zeros((64, 256), F32)
        for dy in (0, *DS):
            ys = minus(y, dy) * N
            if dy:
                for dz in (0, *DS):
                    a_y[p, dz, dy].wait_recv()
            left = jnp.concatenate([ag[p, ys + h] for h in range(N)], axis=1)
            acc += dot(left, xq[pl.ds(ys, N)].reshape(512, 256), ((1,), (0,)))
        tg[p, R] = acc.astype(BF16)

    def spread_t(p, dz):
        block = tg.at[p, x * N + minus(zl, dz)]
        for d in DS:
            t_x[p, dz, d] = send(block, block, at(x=plus(x, d)))

    t_z, t_x = {}, {}
    for dx in (0, *DS):
        x_k[dx].wait_recv()
    for p in range(2):
        project(p)
        for d in DS:
            t_z[p, d] = send(tg.at[p, R], tg.at[p, R], at(zl=plus(zl, d)))
        if p == 0:
            spread_t(0, 0)
    for dz in DS:
        t_z[0, dz].wait_recv()
        spread_t(0, dz)
    spread_t(1, 0)

    @pl.when(turn == 1)
    def _():
        low[0].wait_recv()
        low[0].start()
        low[1].wait_recv()

    @pl.when(turn == 3)
    def _():
        high[1].wait_recv()
        high[1].start()
        high[0].wait_recv()

    for dz in DS:
        t_z[1, dz].wait_recv()
        spread_t(1, dz)

    @pl.when(turn == 2)
    def _():
        low[0].wait_recv()
        high[1].wait_recv()

    line = xp.at[pl.ds(y * N, N)]
    p_y = [send(line, line, at(y=plus(y, d))) for d in DS]
    for copy in p_y:
        copy.wait_recv()

    mine, theirs = pl.ds(k * 128, 128), pl.ds((1 - k) * 128, 128)
    u_x, u_z, o_y, o_z = {}, {}, {}, {}

    def middle(p):
        acc = jnp.zeros((256, 256), F32)
        for dx in (0, *DS):
            xs = minus(x, dx) * N
            if dx:
                for dz in (0, *DS):
                    t_x[p, dz, dx].wait_recv()
            left = xp[pl.ds(xs, N)].reshape(256, 256)
            right = tg[p, pl.ds(xs, N)].reshape(256, 256)
            acc += dot(left, right, ((0,), (0,)))
        gacc[p] = acc
        send(gacc.at[p, theirs], gr.at[p], mate).wait_recv()
        wb[p, mine] = (kv[...] * (gacc[p, mine] + gr[p])).astype(BF16)
        send(wb.at[p, mine], wb.at[p, mine], mate).wait_recv()
        w = wb[p]
        for dx in (*DS, 0):
            xs = plus(x, dx) * N
            part = dot(xp[pl.ds(xs, N)].reshape(256, 256), w, ((1,), (0,))).reshape(N, 64, 256)
            if dx:
                us[p, dx] = part.astype(BF16)
            else:
                us2[p] = part
        for e in (*DS, 0):
            for dx in DS:
                place = us.at[p, dx, plus(zl, e)]
                u_x[p, dx, e] = send(place, urx.at[p, dx, e], at(x=plus(x, dx)))

    def sum_x(p):
        for e in (*DS, 0):
            part = us2[p, plus(zl, e)]
            for dx in DS:
                u_x[p, dx, e].wait_recv()
                part += urx[p, dx, e].astype(F32)
            if e:
                us[p, 0, e] = part.astype(BF16)
                u_z[p, e] = send(us.at[p, 0, e], urz.at[p, e], at(zl=plus(zl, e)))
            else:
                us2[p, zl] = part

    def sum_z(p):
        part = us2[p, zl]
        for e in DS:
            u_z[p, e].wait_recv()
            part += urz[p, e].astype(F32)
        u = part.astype(BF16)
        for dy in (*DS, 0):
            ys = plus(y, dy) * N
            part = dot(u, xq[pl.ds(ys, N)].reshape(512, 256), ((1,), (1,)))
            for h in range(N):
                piece = part[:, h * 128 : h * 128 + 128]
                if dy:
                    osd[p, dy, h] = piece.astype(BF16)
                else:
                    os2[p, h] = piece
        for e in (2, 1, 3, 0):
            for dy in DS:
                place = osd.at[p, dy, plus(zh, e)]
                o_y[p, dy, e] = send(place, ory.at[p, dy, e], at(y=plus(y, dy)))

    def sum_y(p):
        for e in (2, 1, 3, 0):
            part = os2[p, plus(zh, e)]
            for dy in DS:
                o_y[p, dy, e].wait_recv()
                part += ory[p, dy, e].astype(F32)
            if e == 2 or e == (3 if p == 0 else 1):
                osd[p, 0, e] = part.astype(BF16)
                ahead = p == 0 if e == 2 else e == 1
                o_z[p, e] = send(osd.at[p, 0, e], orz.at[p, e], up if ahead else down)
            else:
                os2[p, plus(zh, e)] = part

    def pass_o(p):
        e = 1 if p == 0 else 3
        o_z[p, 2].wait_recv()
        osd[p, 0, e] = (os2[p, plus(zh, e)] + orz[p, 2].astype(F32)).astype(BF16)
        o_z[p, e] = send(osd.at[p, 0, e], orz.at[p, e], up if e == 1 else down)

    def finish(p):
        part = os2[p, zh]
        for e in ((3, 1) if p == 0 else (1, 3)):
            o_z[p, e].wait_recv()
            part += orz[p, e].astype(F32)
        out_ref[p] = part.astype(BF16)

    own_k.wait()
    middle(0)
    middle(1)
    sum_x(0)
    sum_z(0)
    sum_x(1)
    sum_y(0)
    sum_z(1)
    pass_o(0)
    sum_y(1)
    pass_o(1)
    finish(0)
    finish(1)

    for copy in started:
        copy.wait_send()
    for d in DS:
        @pl.when(minus(zl, zh) == d)
        def _():
            collect[d].wait_send()

    @pl.when(root)
    def _():
        for copy in (*low, *high):
            copy.wait_send()

    @pl.when(turn == 1)
    def _():
        low[0].wait_send()

    @pl.when(turn == 3)
    def _():
        high[1].wait_send()


def per_device(amplitudes, factor, kern):
    any_spec = pl.BlockSpec(memory_space=pl.ANY)
    vmem = pltpu.VMEM
    dma = pltpu.SemaphoreType.DMA
    return pl.pallas_call(
        kernel,
        name="ladder",
        out_shape=jax.ShapeDtypeStruct((2, 64, 128), BF16),
        in_specs=[any_spec] * 3,
        out_specs=pl.BlockSpec(memory_space=vmem),
        scratch_shapes=[
            vmem((128, 256), F32),
            vmem((2, 16, 64, 128), BF16),
            vmem((16, 2, 64, 256), BF16),
            vmem((64, 256), BF16),
            vmem((16, 64, 256), BF16),
            vmem((2, 16, 64, 256), BF16),
            vmem((2, 256, 256), F32),
            vmem((2, 128, 256), F32),
            vmem((2, 256, 256), BF16),
            vmem((2, 4, 4, 64, 256), BF16),
            vmem((2, 4, 4, 64, 256), BF16),
            vmem((2, 4, 64, 256), F32),
            vmem((2, 4, 64, 256), BF16),
            vmem((2, 4, 4, 64, 128), BF16),
            vmem((2, 4, 4, 64, 128), BF16),
            vmem((2, 4, 64, 128), F32),
            vmem((2, 4, 64, 128), BF16),
            dma((5,)),
            dma((2, COPIES)),
        ],
        compiler_params=pltpu.CompilerParams(collective_id=0, has_side_effects=True),
    )(amplitudes, factor, kern)


def solution(mesh):
    placed = (P(None, "row", "col"), P("row", "col"), P("row", "col"))
    return jax.shard_map(
        per_device, mesh=mesh, in_specs=placed, out_specs=P(None, "row", "col"), check_vma=False
    )
```

time: 324 us -> 89 us (0.27)
  waiting for transfers between devices: 134 us -> 0 us
  blocking collectives: 130 us -> 0 us
  Pallas kernels: 0 us -> 86.5 us
  starting transfers between devices: 41.1 us -> 0 us
  local copies, waits for them, and re-layouts: 9.69 us -> 1.38 us
  matrix products: 5.35 us -> 0 us
    all_to_all x4 -> x0, waiting for transfers between devices: 134 us -> none  [the longest x3 120 us: sent_to_all(): return lax.all_to_all(copies, axis, split_axis=0, concat_axis=0, tiled=True)]
    all_to_all x3 -> x0, blocking collectives: 130 us -> none  [the longest x2 75.4 us: sent_to_all(): return lax.all_to_all(copies, axis, split_axis=0, concat_axis=0, tiled=True)]
    pallas_call x0 -> x1, Pallas kernels: none -> 86.5 us  [per_device(): pl.pallas_call(kernel, name='ladder', out_shape=jax.ShapeDtypeStruct((2,...]
    all_to_all x4 -> x0, starting transfers between devices: 41.1 us -> none  [the longest x3 34.9 us: sent_to_all(): return lax.all_to_all(copies, axis, split_axis=0, concat_axis=0, tiled=True)]
    broadcast_in_dim x5 -> x0, local copies, waits for them, and re-layouts: 6.2 us -> none  [sent_to_all(): copies = jnp.broadcast_to(value, (lax.axis_size(axis), *value.shape))]
    dot_general x3 -> x0, matrix products: 5.35 us -> none  [the longest x1 3.67 us: per_device(): jnp.einsum('bq,npq->bnp', factor_part, scaled, preferred_element_type=jnp...]
  transfers between devices with their start and end apart: 4 -> 0, of which waited for: 4 -> 0; matrix products, arithmetic and copies ran while one was open for 1% -> 0% of each run, Pallas kernels for 0% -> 0%
where the time goes in v2:
time: 89 us; the launch traced here: 87.9 us
  Pallas kernels  86.5 us (97%)
  local copies, waits for them, and re-layouts  1.38 us (2%)
    pallas_call x1, Pallas kernels, per_device(): pl.pallas_call(kernel, name='ladder', out_shape=jax.ShapeDtypeStruct((2,...  86.5 us

profile of v2, /device:TPU:6, one launch (start us, length us, event | category | flops | bytes accessed | tf_op | source)
XLA Modules:
  0.0 87.9 jit_solution(13386096354441491849)
XLA Ops:
  0.0 86.5 %ladder.1 = bf16[2,64,128]{2,1,0:T(8,128)(2,1)} custom-call(bf16[2,64,128]{2,1,0:T(8,128)(2,1)} %a_ref.1, bf16[64,256]{1,0:T(8,128)(2,1)} %x_ref.1, f32[128,256]{1,0:T(8,128)} %k_ref.1), custom_call_target="tpu_custom_call" | custom-call | tf_op jit(solution)/shard_map/ladder/pallas_call | solution.py:374
  86.5 1.4 %copy.5 = bf16[2,64,128]{2,1,0:T(8,128)(2,1)} copy(bf16[2,64,128]{2,1,0:T(8,128)(2,1)} %ladder.1) | data formatting | bytes 65536

commit v3 on v2

v3 whole, which is shorter than its diff:
```python
import math

import jax
import jax.numpy as jnp
from jax import lax
from jax.experimental import pallas as pl
from jax.experimental.pallas import tpu as pltpu
from jax.sharding import PartitionSpec as P

MESH = pl.DeviceIdType.MESH
F32, BF16 = jnp.float32, jnp.bfloat16
N = 4
DS = (1, 3, 2)
COPIES = 66
UNIT = 64 * 128
UNITS = 290


def dot(a, b, dims):
    return lax.dot_general(a, b, (dims, ((), ())), preferred_element_type=F32)


def kernel(
    a_ref, x_ref, k_ref, out_ref,
    kv, ag, xq, xf, xp, tg, gacc, gr, wb, us, urx, us2, urz, osd, ory, os2, orz, all_sent, lsem, ssem, rsem,
):
    row, col = lax.axis_index("row"), lax.axis_index("col")
    k = lax.rem(row, 2)
    R = lax.div(row, 2)
    x, zl = lax.div(R, N), lax.rem(R, N)
    y, zh = lax.div(col, N), lax.rem(col, N)
    C = col

    def at(x=x, zl=zl, k=k, y=y, zh=zh):
        return ((x * N + zl) * 2 + k, y * N + zh)

    def plus(v, d):
        return lax.rem(v + d, N)

    def minus(v, d):
        return lax.rem(v + N - d, N)

    mate = at(k=1 - k)
    flip = at(x=y, y=x)
    up, down = at(zh=plus(zh, 1)), at(zh=plus(zh, 3))
    swaps = x != y
    root = zl == zh

    used = [0]
    sent = [0]

    def group():
        used[0] += 1
        return used[0] - 1

    def remote(src, dst, device, number, mine=0):
        return pltpu.make_async_remote_copy(
            src_ref=src, dst_ref=dst, send_sem=ssem.at[mine], recv_sem=rsem.at[number],
            device_id=device, device_id_type=MESH,
        )

    def send(src, dst, device, number):
        remote(src, dst, device, number).start()
        sent[0] += math.prod(src.shape) * src.dtype.itemsize // 2 // UNIT

    def arrived(ref, number):
        remote(ref, ref, mate, number).wait_recv()

    def otherwise(condition):
        return pl.when(jnp.logical_not(condition))

    own_a = pltpu.make_async_copy(a_ref, ag.at[:, C], lsem.at[0])
    own_x = pltpu.make_async_copy(x_ref, xq.at[R, k], lsem.at[1])
    own_k = pltpu.make_async_copy(k_ref, kv, lsem.at[2])
    own_f = pltpu.make_async_copy(x_ref, xf, lsem.at[3])
    own_p = pltpu.make_async_copy(xf, xp.at[y * N + zl], lsem.at[4])
    for copy in (own_a, own_x, own_k):
        copy.start()

    barrier = pltpu.get_barrier_semaphore()
    partners = [up, down, mate]
    for d in DS:
        partners += [at(x=plus(x, d)), at(zl=plus(zl, d)), at(y=plus(y, d))]
    for device in partners:
        pl.semaphore_signal(barrier, inc=1, device_id=device, device_id_type=MESH)

    @pl.when(swaps)
    def _():
        pl.semaphore_signal(barrier, inc=1, device_id=flip, device_id_type=MESH)
        pl.semaphore_wait(barrier, len(partners) + 1)

    @otherwise(swaps)
    def _():
        own_f.start()
        pl.semaphore_wait(barrier, len(partners))

    own_a.wait()
    own_x.wait()

    def a_block(p, dz):
        return ag.at[p, y * N + minus(zh, dz)]

    def x_block(dz):
        return xq.at[x * N + minus(zl, dz), k]

    def t_block(p, dz):
        return tg.at[p, x * N + minus(zl, dz)]

    a_ring = {(p, dz): group() for p in range(2) for dz in DS}
    a_y = {(p, d): group() for p in range(2) for d in DS}
    x_z, x_x, x_k = {d: group() for d in DS}, {d: group() for d in DS}, group()
    t_z = {(p, d): group() for p in range(2) for d in DS}
    t_x = {(p, d): group() for p in range(2) for d in DS}
    f_x, f_z, f_y = group(), group(), group()

    def ring_a(p, dz, device, number):
        send(a_block(p, dz), a_block(p, dz), device, a_ring[p, number])

    def spread_a(p, dz):
        for d in DS:
            send(a_block(p, dz), a_block(p, dz), at(y=plus(y, d)), a_y[p, d])

    def spread_x(dz):
        for d in DS:
            send(x_block(dz), x_block(dz), at(x=plus(x, d)), x_x[d])

    def spread_t(p, dz):
        for d in DS:
            send(t_block(p, dz), t_block(p, dz), at(x=plus(x, d)), t_x[p, d])

    def share_x(dx):
        blocks = xq.at[pl.ds(minus(x, dx) * N, N), k]
        send(blocks, blocks, mate, x_k)

    ring_a(0, 0, up, 1)
    ring_a(0, 0, down, 3)
    for d in DS:
        send(x_block(0), x_block(0), at(zl=plus(zl, d)), x_z[d])
    flipped = remote(x_ref, xf, flip, f_x, 1)

    @pl.when(swaps)
    def _():
        flipped.start()

    spread_x(0)
    spread_a(0, 0)
    spread_a(1, 0)
    for dz in DS:
        arrived(x_block(dz), x_z[dz])
        spread_x(dz)
    ring_a(1, 0, down, 3)
    ring_a(1, 0, up, 1)
    arrived(a_block(0, 1), a_ring[0, 1])
    ring_a(0, 1, up, 2)
    spread_a(0, 1)

    @pl.when(swaps)
    def _():
        flipped.wait_send()
        flipped.wait_recv()

    @otherwise(swaps)
    def _():
        own_f.wait()

    collect = remote(xf, xp.at[y * N + zl], at(zl=zh), f_z, 2)

    @pl.when(root)
    def _():
        own_p.start()

    @otherwise(root)
    def _():
        collect.start()

    arrived(a_block(0, 3), a_ring[0, 3])
    spread_a(0, 3)
    share_x(0)

    halves = [xp.at[pl.ds(y * N, 2)], xp.at[pl.ds(y * N + 2, 2)]]
    low = [remote(s, s, up, group(), 3 + i) for i, s in enumerate(halves)]
    high = [remote(s, s, down, group(), 5 + i) for i, s in enumerate(halves)]
    turn = minus(zh, zl)

    @pl.when(root)
    def _():
        own_p.wait()
        arrived(xp.at[pl.ds(0, 3)], f_z)
        low[0].start()
        high[1].start()
        low[1].start()
        high[0].start()

    for dx in DS:
        arrived(xq.at[pl.ds(minus(x, dx) * N, N), k], x_x[dx])
        share_x(dx)
    arrived(a_block(0, 2), a_ring[0, 2])
    spread_a(0, 2)
    arrived(a_block(1, 3), a_ring[1, 3])
    ring_a(1, 3, down, 2)
    spread_a(1, 3)
    arrived(a_block(1, 1), a_ring[1, 1])
    spread_a(1, 1)

    def project(p):
        acc = jnp.zeros((64, 256), F32)
        for dy in (0, *DS):
            ys = minus(y, dy) * N
            if dy:
                arrived(ag.at[p, pl.ds(ys, N)], a_y[p, dy])
            left = jnp.concatenate([ag[p, ys + h] for h in range(N)], axis=1)
            acc += dot(left, xq[pl.ds(ys, N)].reshape(512, 256), ((1,), (0,)))
        tg[p, R] = acc.astype(BF16)
        for d in DS:
            send(t_block(p, 0), t_block(p, 0), at(zl=plus(zl, d)), t_z[p, d])

    arrived(xq.at[:, 1 - k], x_k)
    project(0)
    spread_t(0, 0)

    @pl.when(turn == 1)
    def _():
        low[0].wait_recv()
        low[0].start()
        low[1].wait_recv()

    @pl.when(turn == 3)
    def _():
        high[1].wait_recv()
        high[1].start()
        high[0].wait_recv()

    arrived(a_block(1, 2), a_ring[1, 2])
    spread_a(1, 2)
    for dz in DS:
        arrived(t_block(0, dz), t_z[0, dz])
        spread_t(0, dz)
    project(1)

    @pl.when(turn == 2)
    def _():
        low[0].wait_recv()
        high[1].wait_recv()

    line = xp.at[pl.ds(y * N, N)]
    for d in DS:
        send(line, line, at(y=plus(y, d)), f_y)
    spread_t(1, 0)
    for dz in DS:
        arrived(t_block(1, dz), t_z[1, dz])
        spread_t(1, dz)
    arrived(xp.at[pl.ds(0, 12)], f_y)

    mine, theirs = pl.ds(k * 128, 128), pl.ds((1 - k) * 128, 128)
    back = (*DS, 0)
    to_mate = {(p, i): group() for p in range(2) for i in range(2)}
    u_x = {(p, e): group() for p in range(2) for e in back}
    u_z = {p: group() for p in range(2)}
    o_y = {(p, e): group() for p in range(2) for e in back}
    o_z = {(p, e): group() for p in range(2) for e in DS}

    def middle(p):
        acc = jnp.zeros((256, 256), F32)
        for dx in (0, *DS):
            xs = minus(x, dx) * N
            if dx:
                arrived(tg.at[p, pl.ds(xs, N)], t_x[p, dx])
            left = xp[pl.ds(xs, N)].reshape(256, 256)
            right = tg[p, pl.ds(xs, N)].reshape(256, 256)
            acc += dot(left, right, ((0,), (0,)))
        gacc[p] = acc
        send(gacc.at[p, theirs], gr.at[p], mate, to_mate[p, 0])
        arrived(gr.at[p], to_mate[p, 0])
        wb[p, mine] = (kv[...] * (gacc[p, mine] + gr[p])).astype(BF16)
        send(wb.at[p, mine], wb.at[p, mine], mate, to_mate[p, 1])
        arrived(wb.at[p, theirs], to_mate[p, 1])
        w = wb[p]
        for dx in (*DS, 0):
            xs = plus(x, dx) * N
            part = dot(xp[pl.ds(xs, N)].reshape(256, 256), w, ((1,), (0,))).reshape(N, 64, 256)
            if dx:
                us[p, dx] = part.astype(BF16)
            else:
                us2[p] = part
        for e in (*DS, 0):
            for dx in DS:
                place = us.at[p, dx, plus(zl, e)]
                send(place, urx.at[p, e, dx], at(x=plus(x, dx)), u_x[p, e])

    def sum_x(p):
        for e in (*DS, 0):
            part = us2[p, plus(zl, e)]
            arrived(urx.at[p, e, pl.ds(1, 3)], u_x[p, e])
            for dx in DS:
                part += urx[p, e, dx].astype(F32)
            if e:
                us[p, 0, e] = part.astype(BF16)
                send(us.at[p, 0, e], urz.at[p, e], at(zl=plus(zl, e)), u_z[p])
            else:
                us2[p, zl] = part

    def sum_z(p):
        part = us2[p, zl]
        arrived(urz.at[p, pl.ds(1, 3)], u_z[p])
        for e in DS:
            part += urz[p, e].astype(F32)
        u = part.astype(BF16)
        for dy in (*DS, 0):
            ys = plus(y, dy) * N
            part = dot(u, xq[pl.ds(ys, N)].reshape(512, 256), ((1,), (1,)))
            for h in range(N):
                piece = part[:, h * 128 : h * 128 + 128]
                if dy:
                    osd[p, dy, h] = piece.astype(BF16)
                else:
                    os2[p, h] = piece
        for e in (2, 1, 3, 0):
            for dy in DS:
                place = osd.at[p, dy, plus(zh, e)]
                send(place, ory.at[p, e, dy], at(y=plus(y, dy)), o_y[p, e])

    def sum_y(p):
        for e in (2, 1, 3, 0):
            part = os2[p, plus(zh, e)]
            arrived(ory.at[p, e, pl.ds(1, 3)], o_y[p, e])
            for dy in DS:
                part += ory[p, e, dy].astype(F32)
            if e == 2 or e == (3 if p == 0 else 1):
                osd[p, 0, e] = part.astype(BF16)
                ahead = p == 0 if e == 2 else e == 1
                send(osd.at[p, 0, e], orz.at[p, e], up if ahead else down, o_z[p, e])
            else:
                os2[p, plus(zh, e)] = part

    def pass_o(p):
        e = 1 if p == 0 else 3
        arrived(orz.at[p, 2], o_z[p, 2])
        osd[p, 0, e] = (os2[p, plus(zh, e)] + orz[p, 2].astype(F32)).astype(BF16)
        send(osd.at[p, 0, e], orz.at[p, e], up if e == 1 else down, o_z[p, e])

    def finish(p):
        part = os2[p, zh]
        for e in ((3, 1) if p == 0 else (1, 3)):
            arrived(orz.at[p, e], o_z[p, e])
            part += orz[p, e].astype(F32)
        out_ref[p] = part.astype(BF16)

    own_k.wait()
    middle(0)
    middle(1)
    sum_x(0)
    sum_x(1)
    sum_z(0)
    sum_z(1)
    sum_y(0)
    pass_o(0)
    sum_y(1)
    pass_o(1)
    finish(0)
    finish(1)

    assert sent[0] == UNITS and used[0] <= COPIES, (sent[0], used[0])
    remote(all_sent, all_sent, mate, 0).wait_send()

    @otherwise(root)
    def _():
        collect.wait_send()

    @pl.when(root)
    def _():
        for copy in (*low, *high):
            copy.wait_send()

    @pl.when(turn == 1)
    def _():
        low[0].wait_send()

    @pl.when(turn == 3)
    def _():
        high[1].wait_send()


def per_device(amplitudes, factor, kern):
    any_spec = pl.BlockSpec(memory_space=pl.ANY)
    vmem = pltpu.VMEM
    dma = pltpu.SemaphoreType.DMA
    return pl.pallas_call(
        kernel,
        name="ladder",
        out_shape=jax.ShapeDtypeStruct((2, 64, 128), BF16),
        in_specs=[any_spec] * 3,
        out_specs=pl.BlockSpec(memory_space=vmem),
        scratch_shapes=[
            vmem((128, 256), F32),
            vmem((2, 16, 64, 128), BF16),
            vmem((16, 2, 64, 256), BF16),
            vmem((64, 256), BF16),
            vmem((16, 64, 256), BF16),
            vmem((2, 16, 64, 256), BF16),
            vmem((2, 256, 256), F32),
            vmem((2, 128, 256), F32),
            vmem((2, 256, 256), BF16),
            vmem((2, 4, 4, 64, 256), BF16),
            vmem((2, 4, 4, 64, 256), BF16),
            vmem((2, 4, 64, 256), F32),
            vmem((2, 4, 64, 256), BF16),
            vmem((2, 4, 4, 64, 128), BF16),
            vmem((2, 4, 4, 64, 128), BF16),
            vmem((2, 4, 64, 128), F32),
            vmem((2, 4, 64, 128), BF16),
            vmem((UNITS, 64, 128), BF16),
            dma((5,)),
            dma((7,)),
            dma((COPIES,)),
        ],
        compiler_params=pltpu.CompilerParams(collective_id=0, has_side_effects=True),
    )(amplitudes, factor, kern)


def solution(mesh):
    placed = (P(None, "row", "col"), P("row", "col"), P("row", "col"))
    return jax.shard_map(
        per_device, mesh=mesh, in_specs=placed, out_specs=P(None, "row", "col"), check_vma=False
    )
```

time: 89 us -> 82.2 us (0.924); the launches traced: 87.9 us -> 82 us
  Pallas kernels: 86.5 us -> 80.6 us
    pallas_call x1, Pallas kernels: 86.5 us -> 80.6 us  [per_device(): pl.pallas_call(kernel, name='ladder', out_shape=jax.ShapeDtypeStruct((2,...]
where the time goes in v3:
time: 82.2 us; the launch traced here: 82 us
  Pallas kernels  80.6 us (98%)
  local copies, waits for them, and re-layouts  1.38 us (2%)
    pallas_call x1, Pallas kernels, per_device(): pl.pallas_call(kernel, name='ladder', out_shape=jax.ShapeDtypeStruct((2,...  80.6 us

profile of v3, /device:TPU:6, one launch (start us, length us, event | category | flops | bytes accessed | tf_op | source)
XLA Modules:
  0.0 82.0 jit_solution(3521078733407833905)
XLA Ops:
  0.0 80.6 %ladder.1 = bf16[2,64,128]{2,1,0:T(8,128)(2,1)} custom-call(bf16[2,64,128]{2,1,0:T(8,128)(2,1)} %a_ref.1, bf16[64,256]{1,0:T(8,128)(2,1)} %x_ref.1, f32[128,256]{1,0:T(8,128)} %k_ref.1), custom_call_target="tpu_custom_call" | custom-call | tf_op jit(solution)/shard_map/ladder/pallas_call | solution.py:387
  80.6 1.4 %copy.5 = bf16[2,64,128]{2,1,0:T(8,128)(2,1)} copy(bf16[2,64,128]{2,1,0:T(8,128)(2,1)} %ladder.1) | data formatting | bytes 65536

commit v4 on v3

--- a/solution.py
+++ b/solution.py
@@ -11,7 +11,7 @@
 F32, BF16 = jnp.float32, jnp.bfloat16
 N = 4
 DS = (1, 3, 2)
-COPIES = 66
+COPIES = 86
 UNIT = 64 * 128
 UNITS = 290
 
@@ -103,14 +103,15 @@
     def x_block(dz):
         return xq.at[x * N + minus(zl, dz), k]
 
-    def t_block(p, dz):
-        return tg.at[p, x * N + minus(zl, dz)]
+    def t_block(p, dz, dx=0):
+        return tg.at[p, minus(x, dx) * N + minus(zl, dz)]
 
     a_ring = {(p, dz): group() for p in range(2) for dz in DS}
     a_y = {(p, d): group() for p in range(2) for d in DS}
     x_z, x_x, x_k = {d: group() for d in DS}, {d: group() for d in DS}, group()
     t_z = {(p, d): group() for p in range(2) for d in DS}
-    t_x = {(p, d): group() for p in range(2) for d in DS}
+    t_x = {(p, d, dz): group() for p in range(2) for d in (1, 3) for dz in range(N)}
+    t_far = {p: group() for p in range(2)}
     f_x, f_z, f_y = group(), group(), group()
 
     def ring_a(p, dz, device, number):
@@ -125,8 +126,14 @@
             send(x_block(dz), x_block(dz), at(x=plus(x, d)), x_x[d])
 
     def spread_t(p, dz):
-        for d in DS:
-            send(t_block(p, dz), t_block(p, dz), at(x=plus(x, d)), t_x[p, d])
+        for d in (1, 3):
+            send(t_block(p, dz), t_block(p, dz), at(x=plus(x, d)), t_x[p, d, dz])
+
+    def relay_t(p):
+        for dz, d in ((0, 1), (1, 3), (3, 1), (2, 3)):
+            block = t_block(p, dz, d)
+            arrived(block, t_x[p, d, dz])
+            send(block, block, at(x=plus(x, d)), t_far[p])
 
     def share_x(dx):
         blocks = xq.at[pl.ds(minus(x, dx) * N, N), k]
@@ -222,13 +229,11 @@
     def _():
         low[0].wait_recv()
         low[0].start()
-        low[1].wait_recv()
 
     @pl.when(turn == 3)
     def _():
         high[1].wait_recv()
         high[1].start()
-        high[0].wait_recv()
 
     arrived(a_block(1, 2), a_ring[1, 2])
     spread_a(1, 2)
@@ -236,6 +241,16 @@
         arrived(t_block(0, dz), t_z[0, dz])
         spread_t(0, dz)
     project(1)
+
+    relay_t(0)
+
+    @pl.when(turn == 1)
+    def _():
+        low[1].wait_recv()
+
+    @pl.when(turn == 3)
+    def _():
+        high[0].wait_recv()
 
     @pl.when(turn == 2)
     def _():
@@ -249,22 +264,30 @@
     for dz in DS:
         arrived(t_block(1, dz), t_z[1, dz])
         spread_t(1, dz)
+    relay_t(1)
     arrived(xp.at[pl.ds(0, 12)], f_y)
 
     mine, theirs = pl.ds(k * 128, 128), pl.ds((1 - k) * 128, 128)
     back = (*DS, 0)
     to_mate = {(p, i): group() for p in range(2) for i in range(2)}
     u_x = {(p, e): group() for p in range(2) for e in back}
+    u_far = {(p, e): group() for p in range(2) for e in back}
     u_z = {p: group() for p in range(2)}
     o_y = {(p, e): group() for p in range(2) for e in back}
     o_z = {(p, e): group() for p in range(2) for e in DS}
+
+    via = {0: 1, 3: 1, 1: 3, 2: 3}
 
     def middle(p):
         acc = jnp.zeros((256, 256), F32)
         for dx in (0, *DS):
             xs = minus(x, dx) * N
             if dx:
-                arrived(tg.at[p, pl.ds(xs, N)], t_x[p, dx])
+                for dz, d in ((0, 3), (1, 1), (3, 3), (2, 1)):
+                    if d == dx:
+                        arrived(t_block(p, dz, d), t_x[p, d, dz])
+                if dx == 2:
+                    arrived(tg.at[p, pl.ds(xs, N)], t_far[p])
             left = xp[pl.ds(xs, N)].reshape(256, 256)
             right = tg[p, pl.ds(xs, N)].reshape(256, 256)
             acc += dot(left, right, ((0,), (0,)))
@@ -282,16 +305,24 @@
                 us[p, dx] = part.astype(BF16)
             else:
                 us2[p] = part
-        for e in (*DS, 0):
-            for dx in DS:
-                place = us.at[p, dx, plus(zl, e)]
-                send(place, urx.at[p, e, dx], at(x=plus(x, dx)), u_x[p, e])
+        for e in back:
+            send(us.at[p, 2, plus(zl, e)], urx.at[p, e, 2], at(x=plus(x, via[e])), u_far[p, e])
+        for e in back:
+            d = 4 - via[e]
+            send(us.at[p, d, plus(zl, e)], urx.at[p, e, d], at(x=plus(x, d)), u_x[p, e])
+
+    def relay_u(p):
+        for e in back:
+            d, h = via[e], plus(zl, e)
+            arrived(urx.at[p, e, 2], u_far[p, e])
+            us[p, d, h] = (us[p, d, h].astype(F32) + urx[p, e, 2].astype(F32)).astype(BF16)
+            send(us.at[p, d, h], urx.at[p, e, d], at(x=plus(x, d)), u_x[p, e])
 
     def sum_x(p):
         for e in (*DS, 0):
             part = us2[p, plus(zl, e)]
-            arrived(urx.at[p, e, pl.ds(1, 3)], u_x[p, e])
-            for dx in DS:
+            arrived(urx.at[p, e, pl.ds(0, 2)], u_x[p, e])
+            for dx in (1, 3):
                 part += urx[p, e, dx].astype(F32)
             if e:
                 us[p, 0, e] = part.astype(BF16)
@@ -348,13 +379,15 @@
     own_k.wait()
     middle(0)
     middle(1)
+    relay_u(0)
+    relay_u(1)
     sum_x(0)
     sum_x(1)
     sum_z(0)
     sum_z(1)
     sum_y(0)
+    sum_y(1)
     pass_o(0)
-    sum_y(1)
     pass_o(1)
     finish(0)
     finish(1)

time: 82.2 us -> 80.7 us (0.982); the launches traced: 82 us -> 79.6 us
  Pallas kernels: 80.6 us -> 78.2 us
    pallas_call x1, Pallas kernels: 80.6 us -> 78.2 us  [per_device(): pl.pallas_call(kernel, name='ladder', out_shape=jax.ShapeDtypeStruct((2,...]
where the time goes in v4:
time: 80.7 us; the launch traced here: 79.6 us
  Pallas kernels  78.2 us (97%)
  local copies, waits for them, and re-layouts  1.38 us (2%)
    pallas_call x1, Pallas kernels, per_device(): pl.pallas_call(kernel, name='ladder', out_shape=jax.ShapeDtypeStruct((2,...  78.2 us

profile of v4, /device:TPU:6, one launch (start us, length us, event | category | flops | bytes accessed | tf_op | source)
XLA Modules:
  0.0 79.6 jit_solution(10137868925821296534)
XLA Ops:
  0.0 78.2 %ladder.1 = bf16[2,64,128]{2,1,0:T(8,128)(2,1)} custom-call(bf16[2,64,128]{2,1,0:T(8,128)(2,1)} %a_ref.1, bf16[64,256]{1,0:T(8,128)(2,1)} %x_ref.1, f32[128,256]{1,0:T(8,128)} %k_ref.1), custom_call_target="tpu_custom_call" | custom-call | tf_op jit(solution)/shard_map/ladder/pallas_call | solution.py:420
  78.2 1.4 %copy.5 = bf16[2,64,128]{2,1,0:T(8,128)(2,1)} copy(bf16[2,64,128]{2,1,0:T(8,128)(2,1)} %ladder.1) | data formatting | bytes 65536

commit v5 on v4

--- a/solution.py
+++ b/solution.py
@@ -11,9 +11,9 @@
 F32, BF16 = jnp.float32, jnp.bfloat16
 N = 4
 DS = (1, 3, 2)
-COPIES = 86
+COPIES = 88
 UNIT = 64 * 128
-UNITS = 290
+UNITS = 294
 
 
 def dot(a, b, dims):
@@ -140,9 +140,11 @@
         send(blocks, blocks, mate, x_k)
 
     ring_a(0, 0, up, 1)
-    ring_a(0, 0, down, 3)
+    ring_a(1, 0, down, 3)
     for d in DS:
         send(x_block(0), x_block(0), at(zl=plus(zl, d)), x_z[d])
+    ring_a(0, 0, down, 3)
+    ring_a(1, 0, up, 1)
     flipped = remote(x_ref, xf, flip, f_x, 1)
 
     @pl.when(swaps)
@@ -152,62 +154,59 @@
     spread_x(0)
     spread_a(0, 0)
     spread_a(1, 0)
-    for dz in DS:
-        arrived(x_block(dz), x_z[dz])
-        spread_x(dz)
-    ring_a(1, 0, down, 3)
-    ring_a(1, 0, up, 1)
+    arrived(x_block(1), x_z[1])
+    spread_x(1)
+    arrived(x_block(3), x_z[3])
+    spread_x(3)
+
+    @pl.when(swaps)
+    def _():
+        flipped.wait_send()
+        flipped.wait_recv()
+
+    @otherwise(swaps)
+    def _():
+        own_f.wait()
+
+    place = xp.at[y * N + zl]
+    collect = remote(xf, place, at(zl=zh), f_z, 2)
+    from_below, from_above = [group(), group()], [group(), group()]
+    half = lax.div(zl, 2)
+    halves = [xp.at[pl.ds(y * N, 2)], xp.at[pl.ds(y * N + 2, 2)]]
+    onward_up, onward_down = remote(halves[0], halves[0], up, group(), 3), remote(halves[1], halves[1], down, group(), 4)
+    turn = minus(zh, zl)
+
+    @pl.when(root)
+    def _():
+        own_p.start()
+
+    @otherwise(root)
+    def _():
+        collect.start()
+
+    arrived(x_block(2), x_z[2])
+    spread_x(2)
     arrived(a_block(0, 1), a_ring[0, 1])
     ring_a(0, 1, up, 2)
     spread_a(0, 1)
-
-    @pl.when(swaps)
-    def _():
-        flipped.wait_send()
-        flipped.wait_recv()
-
-    @otherwise(swaps)
-    def _():
-        own_f.wait()
-
-    collect = remote(xf, xp.at[y * N + zl], at(zl=zh), f_z, 2)
-
-    @pl.when(root)
-    def _():
-        own_p.start()
-
-    @otherwise(root)
-    def _():
-        collect.start()
-
+    arrived(a_block(1, 3), a_ring[1, 3])
+    ring_a(1, 3, down, 2)
+    send(xf, place, at(zl=zh, zh=plus(zh, 1)), from_below[0] + half)
+    send(xf, place, at(zl=zh, zh=plus(zh, 3)), from_above[0] + half)
+    spread_a(1, 3)
     arrived(a_block(0, 3), a_ring[0, 3])
     spread_a(0, 3)
+    arrived(a_block(1, 1), a_ring[1, 1])
+    spread_a(1, 1)
     share_x(0)
-
-    halves = [xp.at[pl.ds(y * N, 2)], xp.at[pl.ds(y * N + 2, 2)]]
-    low = [remote(s, s, up, group(), 3 + i) for i, s in enumerate(halves)]
-    high = [remote(s, s, down, group(), 5 + i) for i, s in enumerate(halves)]
-    turn = minus(zh, zl)
-
-    @pl.when(root)
-    def _():
-        own_p.wait()
-        arrived(xp.at[pl.ds(0, 3)], f_z)
-        low[0].start()
-        high[1].start()
-        low[1].start()
-        high[0].start()
 
     for dx in DS:
         arrived(xq.at[pl.ds(minus(x, dx) * N, N), k], x_x[dx])
         share_x(dx)
     arrived(a_block(0, 2), a_ring[0, 2])
     spread_a(0, 2)
-    arrived(a_block(1, 3), a_ring[1, 3])
-    ring_a(1, 3, down, 2)
-    spread_a(1, 3)
-    arrived(a_block(1, 1), a_ring[1, 1])
-    spread_a(1, 1)
+    arrived(a_block(1, 2), a_ring[1, 2])
+    spread_a(1, 2)
 
     def project(p):
         acc = jnp.zeros((64, 256), F32)
@@ -222,48 +221,50 @@
             send(t_block(p, 0), t_block(p, 0), at(zl=plus(zl, d)), t_z[p, d])
 
     arrived(xq.at[:, 1 - k], x_k)
+    @pl.when(turn == 1)
+    def _():
+        arrived(halves[0], from_below[0])
+        onward_up.start()
+
+    @pl.when(turn == 3)
+    def _():
+        arrived(halves[1], from_above[1])
+        onward_down.start()
+
     project(0)
     spread_t(0, 0)
 
-    @pl.when(turn == 1)
-    def _():
-        low[0].wait_recv()
-        low[0].start()
-
-    @pl.when(turn == 3)
-    def _():
-        high[1].wait_recv()
-        high[1].start()
-
-    arrived(a_block(1, 2), a_ring[1, 2])
-    spread_a(1, 2)
+    project(1)
+    spread_t(1, 0)
     for dz in DS:
         arrived(t_block(0, dz), t_z[0, dz])
         spread_t(0, dz)
-    project(1)
-
-    relay_t(0)
+
+    @pl.when(root)
+    def _():
+        own_p.wait()
+        arrived(xp.at[pl.ds(0, 3)], f_z)
 
     @pl.when(turn == 1)
     def _():
-        low[1].wait_recv()
+        arrived(halves[1], from_below[1])
 
     @pl.when(turn == 3)
     def _():
-        high[0].wait_recv()
+        arrived(halves[0], from_above[0])
 
     @pl.when(turn == 2)
     def _():
-        low[0].wait_recv()
-        high[1].wait_recv()
+        onward_up.wait_recv()
+        onward_down.wait_recv()
 
     line = xp.at[pl.ds(y * N, N)]
     for d in DS:
         send(line, line, at(y=plus(y, d)), f_y)
-    spread_t(1, 0)
     for dz in DS:
         arrived(t_block(1, dz), t_z[1, dz])
         spread_t(1, dz)
+    relay_t(0)
     relay_t(1)
     arrived(xp.at[pl.ds(0, 12)], f_y)
 
@@ -278,7 +279,7 @@
 
     via = {0: 1, 3: 1, 1: 3, 2: 3}
 
-    def middle(p):
+    def pairs_part(p):
         acc = jnp.zeros((256, 256), F32)
         for dx in (0, *DS):
             xs = minus(x, dx) * N
@@ -293,9 +294,13 @@
             acc += dot(left, right, ((0,), (0,)))
         gacc[p] = acc
         send(gacc.at[p, theirs], gr.at[p], mate, to_mate[p, 0])
+
+    def scale(p):
         arrived(gr.at[p], to_mate[p, 0])
         wb[p, mine] = (kv[...] * (gacc[p, mine] + gr[p])).astype(BF16)
         send(wb.at[p, mine], wb.at[p, mine], mate, to_mate[p, 1])
+
+    def first_back(p):
         arrived(wb.at[p, theirs], to_mate[p, 1])
         w = wb[p]
         for dx in (*DS, 0):
@@ -377,8 +382,12 @@
         out_ref[p] = part.astype(BF16)
 
     own_k.wait()
-    middle(0)
-    middle(1)
+    pairs_part(0)
+    pairs_part(1)
+    scale(0)
+    scale(1)
+    first_back(0)
+    first_back(1)
     relay_u(0)
     relay_u(1)
     sum_x(0)
@@ -399,18 +408,13 @@
     def _():
         collect.wait_send()
 
-    @pl.when(root)
-    def _():
-        for copy in (*low, *high):
-            copy.wait_send()
-
     @pl.when(turn == 1)
     def _():
-        low[0].wait_send()
+        onward_up.wait_send()
 
     @pl.when(turn == 3)
     def _():
-        high[1].wait_send()
+        onward_down.wait_send()
 
 
 def per_device(amplitudes, factor, kern):
@@ -443,7 +447,7 @@
             vmem((2, 4, 64, 128), BF16),
             vmem((UNITS, 64, 128), BF16),
             dma((5,)),
-            dma((7,)),
+            dma((5,)),
             dma((COPIES,)),
         ],
         compiler_params=pltpu.CompilerParams(collective_id=0, has_side_effects=True),

time: 80.7 us -> 79.6 us (0.986)
  Pallas kernels: 78.2 us -> 77.2 us
    pallas_call x1, Pallas kernels: 78.2 us -> 77.2 us  [per_device(): pl.pallas_call(kernel, name='ladder', out_shape=jax.ShapeDtypeStruct((2,...]
where the time goes in v5:
time: 79.6 us; the launch traced here: 78.5 us
  Pallas kernels  77.2 us (97%)
  local copies, waits for them, and re-layouts  1.38 us (2%)
    pallas_call x1, Pallas kernels, per_device(): pl.pallas_call(kernel, name='ladder', out_shape=jax.ShapeDtypeStruct((2,...  77.2 us

profile of v5, /device:TPU:6, one launch (start us, length us, event | category | flops | bytes accessed | tf_op | source)
XLA Modules:
  0.0 78.5 jit_solution(18165787228055811977)
XLA Ops:
  0.0 77.2 %ladder.1 = bf16[2,64,128]{2,1,0:T(8,128)(2,1)} custom-call(bf16[2,64,128]{2,1,0:T(8,128)(2,1)} %a_ref.1, bf16[64,256]{1,0:T(8,128)(2,1)} %x_ref.1, f32[128,256]{1,0:T(8,128)} %k_ref.1), custom_call_target="tpu_custom_call" | custom-call | tf_op jit(solution)/shard_map/ladder/pallas_call | solution.py:424
  77.2 1.4 %copy.5 = bf16[2,64,128]{2,1,0:T(8,128)(2,1)} copy(bf16[2,64,128]{2,1,0:T(8,128)(2,1)} %ladder.1) | data formatting | bytes 65536

commit v6 on v5

--- a/solution.py
+++ b/solution.py
@@ -11,9 +11,9 @@
 F32, BF16 = jnp.float32, jnp.bfloat16
 N = 4
 DS = (1, 3, 2)
-COPIES = 88
+COPIES = 87
 UNIT = 64 * 128
-UNITS = 294
+UNITS = 310
 
 
 def dot(a, b, dims):
@@ -22,7 +22,7 @@
 
 def kernel(
     a_ref, x_ref, k_ref, out_ref,
-    kv, ag, xq, xf, xp, tg, gacc, gr, wb, us, urx, us2, urz, osd, ory, os2, orz, all_sent, lsem, ssem, rsem,
+    kv, ag, xq, xf, xp, tg, gacc, gr, us, urx, us2, urz, osd, ory, os2, orz, all_sent, lsem, ssem, rsem,
 ):
     row, col = lax.axis_index("row"), lax.axis_index("col")
     k = lax.rem(row, 2)
@@ -71,7 +71,8 @@
 
     own_a = pltpu.make_async_copy(a_ref, ag.at[:, C], lsem.at[0])
     own_x = pltpu.make_async_copy(x_ref, xq.at[R, k], lsem.at[1])
-    own_k = pltpu.make_async_copy(k_ref, kv, lsem.at[2])
+    mine, theirs = pl.ds(k * 128, 128), pl.ds((1 - k) * 128, 128)
+    own_k = pltpu.make_async_copy(k_ref, kv.at[mine], lsem.at[2])
     own_f = pltpu.make_async_copy(x_ref, xf, lsem.at[3])
     own_p = pltpu.make_async_copy(xf, xp.at[y * N + zl], lsem.at[4])
     for copy in (own_a, own_x, own_k):
@@ -96,6 +97,8 @@
 
     own_a.wait()
     own_x.wait()
+    own_k.wait()
+    mate_k = group()
 
     def a_block(p, dz):
         return ag.at[p, y * N + minus(zh, dz)]
@@ -199,6 +202,7 @@
     arrived(a_block(1, 1), a_ring[1, 1])
     spread_a(1, 1)
     share_x(0)
+    send(kv.at[mine], kv.at[mine], mate, mate_k)
 
     for dx in DS:
         arrived(xq.at[pl.ds(minus(x, dx) * N, N), k], x_x[dx])
@@ -207,6 +211,16 @@
     spread_a(0, 2)
     arrived(a_block(1, 2), a_ring[1, 2])
     spread_a(1, 2)
+
+    @pl.when(turn == 1)
+    def _():
+        arrived(halves[0], from_below[0])
+        onward_up.start()
+
+    @pl.when(turn == 3)
+    def _():
+        arrived(halves[1], from_above[1])
+        onward_down.start()
 
     def project(p):
         acc = jnp.zeros((64, 256), F32)
@@ -221,19 +235,8 @@
             send(t_block(p, 0), t_block(p, 0), at(zl=plus(zl, d)), t_z[p, d])
 
     arrived(xq.at[:, 1 - k], x_k)
-    @pl.when(turn == 1)
-    def _():
-        arrived(halves[0], from_below[0])
-        onward_up.start()
-
-    @pl.when(turn == 3)
-    def _():
-        arrived(halves[1], from_above[1])
-        onward_down.start()
-
     project(0)
     spread_t(0, 0)
-
     project(1)
     spread_t(1, 0)
     for dz in DS:
@@ -268,9 +271,8 @@
     relay_t(1)
     arrived(xp.at[pl.ds(0, 12)], f_y)
 
-    mine, theirs = pl.ds(k * 128, 128), pl.ds((1 - k) * 128, 128)
     back = (*DS, 0)
-    to_mate = {(p, i): group() for p in range(2) for i in range(2)}
+    to_mate = {p: group() for p in range(2)}
     u_x = {(p, e): group() for p in range(2) for e in back}
     u_far = {(p, e): group() for p in range(2) for e in back}
     u_z = {p: group() for p in range(2)}
@@ -293,16 +295,11 @@
             right = tg[p, pl.ds(xs, N)].reshape(256, 256)
             acc += dot(left, right, ((0,), (0,)))
         gacc[p] = acc
-        send(gacc.at[p, theirs], gr.at[p], mate, to_mate[p, 0])
-
-    def scale(p):
-        arrived(gr.at[p], to_mate[p, 0])
-        wb[p, mine] = (kv[...] * (gacc[p, mine] + gr[p])).astype(BF16)
-        send(wb.at[p, mine], wb.at[p, mine], mate, to_mate[p, 1])
+        send(gacc.at[p], gr.at[p], mate, to_mate[p])
 
     def first_back(p):
-        arrived(wb.at[p, theirs], to_mate[p, 1])
-        w = wb[p]
+        arrived(gr.at[p], to_mate[p])
+        w = (kv[...] * (gacc[p] + gr[p])).astype(BF16)
         for dx in (*DS, 0):
             xs = plus(x, dx) * N
             part = dot(xp[pl.ds(xs, N)].reshape(256, 256), w, ((1,), (0,))).reshape(N, 64, 256)
@@ -350,23 +347,23 @@
                     osd[p, dy, h] = piece.astype(BF16)
                 else:
                     os2[p, h] = piece
-        for e in (2, 1, 3, 0):
-            for dy in DS:
-                place = osd.at[p, dy, plus(zh, e)]
-                send(place, ory.at[p, e, dy], at(y=plus(y, dy)), o_y[p, e])
-
-    def sum_y(p):
-        for e in (2, 1, 3, 0):
-            part = os2[p, plus(zh, e)]
-            arrived(ory.at[p, e, pl.ds(1, 3)], o_y[p, e])
-            for dy in DS:
-                part += ory[p, e, dy].astype(F32)
-            if e == 2 or e == (3 if p == 0 else 1):
-                osd[p, 0, e] = part.astype(BF16)
-                ahead = p == 0 if e == 2 else e == 1
-                send(osd.at[p, 0, e], orz.at[p, e], up if ahead else down, o_z[p, e])
-            else:
-                os2[p, plus(zh, e)] = part
+
+    def spread_o(p, e):
+        for dy in DS:
+            place = osd.at[p, dy, plus(zh, e)]
+            send(place, ory.at[p, e, dy], at(y=plus(y, dy)), o_y[p, e])
+
+    def sum_y(p, e):
+        part = os2[p, plus(zh, e)]
+        arrived(ory.at[p, e, pl.ds(1, 3)], o_y[p, e])
+        for dy in DS:
+            part += ory[p, e, dy].astype(F32)
+        if e == 2 or e == (3 if p == 0 else 1):
+            osd[p, 0, e] = part.astype(BF16)
+            ahead = p == 0 if e == 2 else e == 1
+            send(osd.at[p, 0, e], orz.at[p, e], up if ahead else down, o_z[p, e])
+        else:
+            os2[p, plus(zh, e)] = part
 
     def pass_o(p):
         e = 1 if p == 0 else 3
@@ -381,11 +378,9 @@
             part += orz[p, e].astype(F32)
         out_ref[p] = part.astype(BF16)
 
-    own_k.wait()
+    arrived(kv.at[theirs], mate_k)
     pairs_part(0)
     pairs_part(1)
-    scale(0)
-    scale(1)
     first_back(0)
     first_back(1)
     relay_u(0)
@@ -393,11 +388,25 @@
     sum_x(0)
     sum_x(1)
     sum_z(0)
+    spread_o(0, 2)
+    spread_o(0, 1)
     sum_z(1)
-    sum_y(0)
-    sum_y(1)
+    spread_o(1, 2)
+    spread_o(1, 3)
+    spread_o(0, 3)
+    spread_o(1, 1)
+    spread_o(0, 0)
+    spread_o(1, 0)
+    sum_y(0, 2)
+    sum_y(0, 1)
+    sum_y(1, 2)
+    sum_y(1, 3)
+    sum_y(0, 3)
+    sum_y(1, 1)
     pass_o(0)
     pass_o(1)
+    sum_y(0, 0)
+    sum_y(1, 0)
     finish(0)
     finish(1)
 
@@ -424,19 +433,18 @@
     return pl.pallas_call(
         kernel,
         name="ladder",
-        out_shape=jax.ShapeDtypeStruct((2, 64, 128), BF16),
+        out_shape=pltpu.VMEM((2, 64, 128), BF16),
         in_specs=[any_spec] * 3,
         out_specs=pl.BlockSpec(memory_space=vmem),
         scratch_shapes=[
-            vmem((128, 256), F32),
+            vmem((256, 256), F32),
             vmem((2, 16, 64, 128), BF16),
             vmem((16, 2, 64, 256), BF16),
             vmem((64, 256), BF16),
             vmem((16, 64, 256), BF16),
             vmem((2, 16, 64, 256), BF16),
             vmem((2, 256, 256), F32),
-            vmem((2, 128, 256), F32),
-            vmem((2, 256, 256), BF16),
+            vmem((2, 256, 256), F32),
             vmem((2, 4, 4, 64, 256), BF16),
             vmem((2, 4, 4, 64, 256), BF16),
             vmem((2, 4, 64, 256), F32),

time: 79.6 us -> 77.6 us (0.975)
  the two profiles are of different devices: /device:TPU:6 before, /device:TPU:4 now
where the time goes in v6:
time: 77.6 us; the launch traced here: 77.4 us
  Pallas kernels  76.8 us (99%)
    pallas_call x1, Pallas kernels, per_device(): pl.pallas_call(kernel, name='ladder', out_shape=pltpu.VMEM((2, 64, 128),...  76.8 us

profile of v6, /device:TPU:4, one launch (start us, length us, event | category | flops | bytes accessed | tf_op | source)
XLA Modules:
  0.0 77.4 jit_solution(8142156252129276287)
XLA Ops:
  0.0 76.8 %ladder.1 = bf16[2,64,128]{2,1,0:T(8,128)(2,1)S(1)} custom-call(bf16[2,64,128]{2,1,0:T(8,128)(2,1)} %a_ref.1, bf16[64,256]{1,0:T(8,128)(2,1)} %x_ref.1, f32[128,256]{1,0:T(8,128)} %k_ref.1), custom_call_target="tpu_custom_call" | custom-call | tf_op jit(solution)/shard_map/ladder/pallas_call | solution.py:433
  76.8 0.6 copy.5

commit v7 on v6

--- a/solution.py
+++ b/solution.py
@@ -11,7 +11,8 @@
 F32, BF16 = jnp.float32, jnp.bfloat16
 N = 4
 DS = (1, 3, 2)
-COPIES = 87
+SUMS = ((0, 2), (0, 1), (1, 2), (1, 3), (0, 3), (1, 1), (0, 0), (1, 0))
+COPIES = 71
 UNIT = 64 * 128
 UNITS = 310
 
@@ -113,8 +114,7 @@
     a_y = {(p, d): group() for p in range(2) for d in DS}
     x_z, x_x, x_k = {d: group() for d in DS}, {d: group() for d in DS}, group()
     t_z = {(p, d): group() for p in range(2) for d in DS}
-    t_x = {(p, d, dz): group() for p in range(2) for d in (1, 3) for dz in range(N)}
-    t_far = {p: group() for p in range(2)}
+    t_x = {(p, d): group() for p in range(2) for d in DS}
     f_x, f_z, f_y = group(), group(), group()
 
     def ring_a(p, dz, device, number):
@@ -129,14 +129,8 @@
             send(x_block(dz), x_block(dz), at(x=plus(x, d)), x_x[d])
 
     def spread_t(p, dz):
-        for d in (1, 3):
-            send(t_block(p, dz), t_block(p, dz), at(x=plus(x, d)), t_x[p, d, dz])
-
-    def relay_t(p):
-        for dz, d in ((0, 1), (1, 3), (3, 1), (2, 3)):
-            block = t_block(p, dz, d)
-            arrived(block, t_x[p, d, dz])
-            send(block, block, at(x=plus(x, d)), t_far[p])
+        for d in DS:
+            send(t_block(p, dz), t_block(p, dz), at(x=plus(x, d)), t_x[p, d])
 
     def share_x(dx):
         blocks = xq.at[pl.ds(minus(x, dx) * N, N), k]
@@ -267,8 +261,6 @@
     for dz in DS:
         arrived(t_block(1, dz), t_z[1, dz])
         spread_t(1, dz)
-    relay_t(0)
-    relay_t(1)
     arrived(xp.at[pl.ds(0, 12)], f_y)
 
     back = (*DS, 0)
@@ -277,7 +269,7 @@
     u_far = {(p, e): group() for p in range(2) for e in back}
     u_z = {p: group() for p in range(2)}
     o_y = {(p, e): group() for p in range(2) for e in back}
-    o_z = {(p, e): group() for p in range(2) for e in DS}
+    o_z = {p: group() for p in range(2)}
 
     via = {0: 1, 3: 1, 1: 3, 2: 3}
 
@@ -286,11 +278,7 @@
         for dx in (0, *DS):
             xs = minus(x, dx) * N
             if dx:
-                for dz, d in ((0, 3), (1, 1), (3, 3), (2, 1)):
-                    if d == dx:
-                        arrived(t_block(p, dz, d), t_x[p, d, dz])
-                if dx == 2:
-                    arrived(tg.at[p, pl.ds(xs, N)], t_far[p])
+                arrived(tg.at[p, pl.ds(xs, N)], t_x[p, dx])
             left = xp[pl.ds(xs, N)].reshape(256, 256)
             right = tg[p, pl.ds(xs, N)].reshape(256, 256)
             acc += dot(left, right, ((0,), (0,)))
@@ -358,23 +346,16 @@
         arrived(ory.at[p, e, pl.ds(1, 3)], o_y[p, e])
         for dy in DS:
             part += ory[p, e, dy].astype(F32)
-        if e == 2 or e == (3 if p == 0 else 1):
+        if e:
             osd[p, 0, e] = part.astype(BF16)
-            ahead = p == 0 if e == 2 else e == 1
-            send(osd.at[p, 0, e], orz.at[p, e], up if ahead else down, o_z[p, e])
+            send(osd.at[p, 0, e], orz.at[p, e], at(zh=plus(zh, e)), o_z[p])
         else:
-            os2[p, plus(zh, e)] = part
-
-    def pass_o(p):
-        e = 1 if p == 0 else 3
-        arrived(orz.at[p, 2], o_z[p, 2])
-        osd[p, 0, e] = (os2[p, plus(zh, e)] + orz[p, 2].astype(F32)).astype(BF16)
-        send(osd.at[p, 0, e], orz.at[p, e], up if e == 1 else down, o_z[p, e])
+            os2[p, zh] = part
 
     def finish(p):
         part = os2[p, zh]
-        for e in ((3, 1) if p == 0 else (1, 3)):
-            arrived(orz.at[p, e], o_z[p, e])
+        arrived(orz.at[p, pl.ds(1, 3)], o_z[p])
+        for e in DS:
             part += orz[p, e].astype(F32)
         out_ref[p] = part.astype(BF16)
 
@@ -391,22 +372,10 @@
     spread_o(0, 2)
     spread_o(0, 1)
     sum_z(1)
-    spread_o(1, 2)
-    spread_o(1, 3)
-    spread_o(0, 3)
-    spread_o(1, 1)
-    spread_o(0, 0)
-    spread_o(1, 0)
-    sum_y(0, 2)
-    sum_y(0, 1)
-    sum_y(1, 2)
-    sum_y(1, 3)
-    sum_y(0, 3)
-    sum_y(1, 1)
-    pass_o(0)
-    pass_o(1)
-    sum_y(0, 0)
-    sum_y(1, 0)
+    for p, e in SUMS[2:]:
+        spread_o(p, e)
+    for p, e in SUMS:
+        sum_y(p, e)
     finish(0)
     finish(1)
 

time: 77.6 us -> 73.8 us (0.951)
  the two profiles are of different devices: /device:TPU:4 before, /device:TPU:6 now
where the time goes in v7:
time: 73.8 us; the launch traced here: 72.9 us
  Pallas kernels  72.3 us (98%)
    pallas_call x1, Pallas kernels, per_device(): pl.pallas_call(kernel, name='ladder', out_shape=pltpu.VMEM((2, 64, 128),...  72.3 us

profile of v7, /device:TPU:6, one launch (start us, length us, event | category | flops | bytes accessed | tf_op | source)
XLA Modules:
  0.0 72.9 jit_solution(2215880523636451652)
XLA Ops:
  0.0 72.3 %ladder.1 = bf16[2,64,128]{2,1,0:T(8,128)(2,1)S(1)} custom-call(bf16[2,64,128]{2,1,0:T(8,128)(2,1)} %a_ref.1, bf16[64,256]{1,0:T(8,128)(2,1)} %x_ref.1, f32[128,256]{1,0:T(8,128)} %k_ref.1), custom_call_target="tpu_custom_call" | custom-call | tf_op jit(solution)/shard_map/ladder/pallas_call | solution.py:402
  72.3 0.6 copy.5

commit v8 on v7

--- a/solution.py
+++ b/solution.py
@@ -138,10 +138,10 @@
 
     ring_a(0, 0, up, 1)
     ring_a(1, 0, down, 3)
+    ring_a(0, 0, down, 3)
+    ring_a(1, 0, up, 1)
     for d in DS:
         send(x_block(0), x_block(0), at(zl=plus(zl, d)), x_z[d])
-    ring_a(0, 0, down, 3)
-    ring_a(1, 0, up, 1)
     flipped = remote(x_ref, xf, flip, f_x, 1)
 
     @pl.when(swaps)
@@ -206,6 +206,20 @@
     arrived(a_block(1, 2), a_ring[1, 2])
     spread_a(1, 2)
 
+    line = xp.at[pl.ds(y * N, N)]
+
+    def spread_p(blocks):
+        for d in DS:
+            remote(blocks, blocks, at(y=plus(y, d)), f_y).start()
+
+    sent[0] += 3 * math.prod(line.shape) // UNIT
+
+    @pl.when(root)
+    def _():
+        own_p.wait()
+        arrived(xp.at[pl.ds(0, 3)], f_z)
+        spread_p(line)
+
     @pl.when(turn == 1)
     def _():
         arrived(halves[0], from_below[0])
@@ -231,33 +245,30 @@
     arrived(xq.at[:, 1 - k], x_k)
     project(0)
     spread_t(0, 0)
+
+    @pl.when(turn == 1)
+    def _():
+        arrived(halves[1], from_below[1])
+        spread_p(line)
+
+    @pl.when(turn == 3)
+    def _():
+        arrived(halves[0], from_above[0])
+        spread_p(line)
+
     project(1)
     spread_t(1, 0)
     for dz in DS:
         arrived(t_block(0, dz), t_z[0, dz])
         spread_t(0, dz)
-
-    @pl.when(root)
-    def _():
-        own_p.wait()
-        arrived(xp.at[pl.ds(0, 3)], f_z)
-
-    @pl.when(turn == 1)
-    def _():
-        arrived(halves[1], from_below[1])
-
-    @pl.when(turn == 3)
-    def _():
-        arrived(halves[0], from_above[0])
-
-    @pl.when(turn == 2)
-    def _():
-        onward_up.wait_recv()
-        onward_down.wait_recv()
-
-    line = xp.at[pl.ds(y * N, N)]
-    for d in DS:
-        send(line, line, at(y=plus(y, d)), f_y)
+        if dz == 1:
+            @pl.when(turn == 2)
+            def _():
+                onward_up.wait_recv()
+                spread_p(halves[0])
+                onward_down.wait_recv()
+                spread_p(halves[1])
+
     for dz in DS:
         arrived(t_block(1, dz), t_z[1, dz])
         spread_t(1, dz)

time: 73.8 us -> 73.3 us (level)
  the two profiles are of different devices: /device:TPU:6 before, /device:TPU:8 now
where the time goes in v8:
time: 73.3 us; the launch traced here: 73.2 us
  Pallas kernels  72.5 us (99%)
    pallas_call x1, Pallas kernels, per_device(): pl.pallas_call(kernel, name='ladder', out_shape=pltpu.VMEM((2, 64, 128),...  72.5 us

profile of v8, /device:TPU:8, one launch (start us, length us, event | category | flops | bytes accessed | tf_op | source)
XLA Modules:
  0.0 73.2 jit_solution(5746364805867033080)
XLA Ops:
  0.0 72.5 %ladder.1 = bf16[2,64,128]{2,1,0:T(8,128)(2,1)S(1)} custom-call(bf16[2,64,128]{2,1,0:T(8,128)(2,1)} %a_ref.1, bf16[64,256]{1,0:T(8,128)(2,1)} %x_ref.1, f32[128,256]{1,0:T(8,128)} %k_ref.1), custom_call_target="tpu_custom_call" | custom-call | tf_op jit(solution)/shard_map/ladder/pallas_call | solution.py:413
  72.5 0.6 copy.5

commit v9 on v8

--- a/solution.py
+++ b/solution.py
@@ -125,6 +125,7 @@
             send(a_block(p, dz), a_block(p, dz), at(y=plus(y, d)), a_y[p, d])
 
     def spread_x(dz):
+        send(x_block(dz), x_block(dz), mate, x_k)
         for d in DS:
             send(x_block(dz), x_block(dz), at(x=plus(x, d)), x_x[d])
 
@@ -195,7 +196,6 @@
     spread_a(0, 3)
     arrived(a_block(1, 1), a_ring[1, 1])
     spread_a(1, 1)
-    share_x(0)
     send(kv.at[mine], kv.at[mine], mate, mate_k)
 
     for dx in DS:
@@ -299,18 +299,19 @@
     def first_back(p):
         arrived(gr.at[p], to_mate[p])
         w = (kv[...] * (gacc[p] + gr[p])).astype(BF16)
-        for dx in (*DS, 0):
+        for dx in (2, 1, 3, 0):
             xs = plus(x, dx) * N
             part = dot(xp[pl.ds(xs, N)].reshape(256, 256), w, ((1,), (0,))).reshape(N, 64, 256)
-            if dx:
-                us[p, dx] = part.astype(BF16)
-            else:
+            if dx == 0:
                 us2[p] = part
-        for e in back:
-            send(us.at[p, 2, plus(zl, e)], urx.at[p, e, 2], at(x=plus(x, via[e])), u_far[p, e])
-        for e in back:
-            d = 4 - via[e]
-            send(us.at[p, d, plus(zl, e)], urx.at[p, e, d], at(x=plus(x, d)), u_x[p, e])
+                continue
+            us[p, dx] = part.astype(BF16)
+            for e in back:
+                block = us.at[p, dx, plus(zl, e)]
+                if dx == 2:
+                    send(block, urx.at[p, e, 2], at(x=plus(x, via[e])), u_far[p, e])
+                elif dx != via[e]:
+                    send(block, urx.at[p, e, dx], at(x=plus(x, dx)), u_x[p, e])
 
     def relay_u(p):
         for e in back:

time: 73.3 us -> 73.2 us (level)
  no operation moved by 1% of the time
where the time goes in v9:
time: 73.2 us; the launch traced here: 73.1 us
  Pallas kernels  72.4 us (99%)
    pallas_call x1, Pallas kernels, per_device(): pl.pallas_call(kernel, name='ladder', out_shape=pltpu.VMEM((2, 64, 128),...  72.4 us

profile of v9, /device:TPU:8, one launch (start us, length us, event | category | flops | bytes accessed | tf_op | source)
XLA Modules:
  0.0 73.1 jit_solution(6104891713396901128)
XLA Ops:
  0.0 72.4 %ladder.1 = bf16[2,64,128]{2,1,0:T(8,128)(2,1)S(1)} custom-call(bf16[2,64,128]{2,1,0:T(8,128)(2,1)} %a_ref.1, bf16[64,256]{1,0:T(8,128)(2,1)} %x_ref.1, f32[128,256]{1,0:T(8,128)} %k_ref.1), custom_call_target="tpu_custom_call" | custom-call | tf_op jit(solution)/shard_map/ladder/pallas_call | solution.py:414
  72.5 0.6 copy.5

commit v10 on v9

--- a/solution.py
+++ b/solution.py
@@ -154,6 +154,11 @@
     spread_a(1, 0)
     arrived(x_block(1), x_z[1])
     spread_x(1)
+    arrived(a_block(0, 1), a_ring[0, 1])
+    ring_a(0, 1, up, 2)
+    spread_a(0, 1)
+    arrived(a_block(1, 3), a_ring[1, 3])
+    ring_a(1, 3, down, 2)
     arrived(x_block(3), x_z[3])
     spread_x(3)
 
@@ -184,11 +189,6 @@
 
     arrived(x_block(2), x_z[2])
     spread_x(2)
-    arrived(a_block(0, 1), a_ring[0, 1])
-    ring_a(0, 1, up, 2)
-    spread_a(0, 1)
-    arrived(a_block(1, 3), a_ring[1, 3])
-    ring_a(1, 3, down, 2)
     send(xf, place, at(zl=zh, zh=plus(zh, 1)), from_below[0] + half)
     send(xf, place, at(zl=zh, zh=plus(zh, 3)), from_above[0] + half)
     spread_a(1, 3)
@@ -332,6 +332,10 @@
             else:
                 us2[p, zl] = part
 
+    def send_o(p, e, dy):
+        place = osd.at[p, dy, plus(zh, e)]
+        send(place, ory.at[p, e, dy], at(y=plus(y, dy)), o_y[p, e])
+
     def sum_z(p):
         part = us2[p, zl]
         arrived(urz.at[p, pl.ds(1, 3)], u_z[p])
@@ -347,11 +351,12 @@
                     osd[p, dy, h] = piece.astype(BF16)
                 else:
                     os2[p, h] = piece
+            if dy:
+                send_o(p, 2, dy)
 
     def spread_o(p, e):
         for dy in DS:
-            place = osd.at[p, dy, plus(zh, e)]
-            send(place, ory.at[p, e, dy], at(y=plus(y, dy)), o_y[p, e])
+            send_o(p, e, dy)
 
     def sum_y(p, e):
         part = os2[p, plus(zh, e)]
@@ -381,10 +386,9 @@
     sum_x(0)
     sum_x(1)
     sum_z(0)
-    spread_o(0, 2)
     spread_o(0, 1)
     sum_z(1)
-    for p, e in SUMS[2:]:
+    for p, e in SUMS[3:]:
         spread_o(p, e)
     for p, e in SUMS:
         sum_y(p, e)

time: 73.2 us -> 73 us (level)
  the two profiles are of different devices: /device:TPU:8 before, /device:TPU:6 now
where the time goes in v10:
time: 73 us; the launch traced here: 71.7 us
  Pallas kernels  71.1 us (97%)
    pallas_call x1, Pallas kernels, per_device(): pl.pallas_call(kernel, name='ladder', out_shape=pltpu.VMEM((2, 64, 128),...  71.1 us

profile of v10, /device:TPU:6, one launch (start us, length us, event | category | flops | bytes accessed | tf_op | source)
XLA Modules:
  0.0 71.7 jit_solution(16687531471227256655)
XLA Ops:
  0.0 71.1 %ladder.1 = bf16[2,64,128]{2,1,0:T(8,128)(2,1)S(1)} custom-call(bf16[2,64,128]{2,1,0:T(8,128)(2,1)} %a_ref.1, bf16[64,256]{1,0:T(8,128)(2,1)} %x_ref.1, f32[128,256]{1,0:T(8,128)} %k_ref.1), custom_call_target="tpu_custom_call" | custom-call | tf_op jit(solution)/shard_map/ladder/pallas_call | solution.py:418
  71.1 0.6 copy.5
